TPU v7x, 256 devices: a whole 4x4x8 slice. The times are simulated.
256 devices in a mesh: ctx: 32 (over y, z), head: 8 (over x, core).
Axes of the slice: x: 4, y: 4, z: 8, core: 2. Of those that a mesh axis runs over, the one named last changes fastest.
Arguments:
- queries: bfloat16 [32768, 4096], P('ctx', 'head'), as said below
- key_value: bfloat16 [2, 32768, 4096], P(None, 'ctx', 'head'), as said below
- lanczos_vec: float32 [32768, 4096], P('ctx', 'head'), as said below
- rand_blocks: int32 [256, 3], replicated, may hold values from 0 to 255, as said below
- global_ids: int32 [2], replicated, may hold values from 0 to 255
Outputs:
- next_vec: float32 [32768, 4096], P('ctx', 'head')
- coefficients: float32 [2], replicated
Inputs may be any that keep to these rules, and one draw needn't show every extreme that they name: `rand_blocks`: row b lists the random key blocks of query block b. For each shard of 8 query blocks along ctx and each shard of 8 key blocks, at most 1 of the shard's listed random blocks lie in that key shard, and every query shard reaches 1 with some key shard. `queries`: entries are of order one or a few tens. `key_value`: keys of order one, values of order one to a few hundred. `lanczos_vec`: nonzero real entries; the mean of their squares over all entries is one, up to float32 rounding.
All inputs are finite; a program needn't handle non-finite values.
Results may differ from a plain program's by a relative error of at most 0.0049.
Values may be sent and summed in bfloat16 or wider, within the bound.
No kernel may reach another device: no remote copies, remote signals or barrier semaphores. Data moves between devices by JAX's collectives and lax.ppermute only.
A program may use at most 128 MiB of HBM per device.

v0:
```python
import functools

import jax
import jax.numpy as jnp
from jax import lax
from jax.experimental import pallas as pl
from jax.experimental.pallas import tpu as pltpu
from jax.sharding import PartitionSpec as P


HD = 128
BS = 128
LIST = 8
SCALE = HD ** (-0.5)
LOG2E = 1.4426950408889634
NT = (((1,), (1,)), ((), ()))


def attend_tile(q, tangent, keys, values, left_bias, right_bias):
    both = jnp.concatenate([q, tangent], axis=0)
    logits = lax.dot_general(both, keys, NT, preferred_element_type=jnp.float32)
    scores = logits[:BS]
    dots = logits[BS:]
    scores = jnp.concatenate(
        [
            scores[:, :BS] + left_bias,
            scores[:, BS : 2 * BS],
            scores[:, 2 * BS : 3 * BS] + right_bias,
            scores[:, 3 * BS :],
        ],
        axis=1,
    )
    row_top = jnp.max(scores, axis=1, keepdims=True)
    weights = jnp.exp2((scores - row_top) * (SCALE * LOG2E))
    inv_total = 1.0 / jnp.sum(weights, axis=1, keepdims=True)
    prob = weights * inv_total
    center = jnp.sum(prob * dots, axis=1, keepdims=True)
    first = ((prob * SCALE) * (dots - center)).astype(jnp.bfloat16)
    dout = jnp.dot(first, values, preferred_element_type=jnp.float32).astype(jnp.bfloat16)
    dprob = lax.dot_general(dout, values, NT, preferred_element_type=jnp.float32)
    center_two = jnp.sum(prob * dprob, axis=1, keepdims=True)
    second = (prob * (dprob - center_two)).astype(jnp.bfloat16)
    return jnp.dot(second, keys, preferred_element_type=jnp.float32) * SCALE


NY, NZ = 4, 8
CHUNKS = ((0, 2), (2, 2))
CALLS = len(CHUNKS)
OWN, L1, _, _, _, _, _, R1, YP, YM, _, LYP, _, _, MP, _, _ = range(17)


def start_choice(arrays, ids, code, dst, sem):
    which = lax.shift_right_logical(code, 3)
    slot = code & 7
    for k in ids:
        @pl.when(which == k)
        def _(k=k):
            pltpu.make_async_copy(arrays[k].at[slot], dst, sem).start()


def attention_kernel(nblocks, chunk, narrays, code_ref, q_ref, vec_ref, *refs):
    arrays = refs[:narrays]
    pieces = refs[narrays : narrays + NY]
    out_ref, stat_ref, kvbuf, sems, acc = refs[narrays + NY :]
    b = pl.program_id(0)
    width = q_ref.shape[1]
    table = nblocks * 6
    listed = (0, 1, 2, 5, 6, 7)

    def place(slot, pos):
        return kvbuf.at[slot, :, pl.ds(pos * BS, BS)]

    def globals_in(slot):
        copies = []
        cols = pl.ds(chunk[0] * HD, width)
        for i in range(NY):
            rows = pl.multiple_of(code_ref[table + 2 + i], BS // NY)
            for g in range(2):
                dst = kvbuf.at[slot, :, pl.ds((3 + g) * BS + rows, BS // NY)]
                sem = sems.at[slot, LIST + 2 * i + g]
                copies.append(pltpu.make_async_copy(pieces[i].at[g, :, :, cols], dst, sem))
        return copies

    def start(blk, slot):
        for j, pos in enumerate(listed):
            ids = (
                (OWN, L1, YP) if pos == 0 else (OWN,) if pos == 1 else (OWN, R1, YM) if pos == 2
                else tuple(range(narrays))
            )
            start_choice(arrays, ids, code_ref[blk * 6 + j], place(slot, pos), sems.at[slot, pos])

        @pl.when(blk < 2)
        def _():
            for cp in globals_in(slot):
                cp.start()

    slot = lax.rem(b, 2)

    @pl.when(b == 0)
    def _():
        start(0, 0)

    @pl.when(b + 1 < nblocks)
    def _():
        start(b + 1, 1 - slot)

    for pos in listed:
        pltpu.make_async_copy(arrays[OWN].at[0], place(slot, pos), sems.at[slot, pos]).wait()

    @pl.when(b < 2)
    def _():
        for cp in globals_in(slot):
            cp.wait()

    left_bias = jnp.where((b == 0) & (code_ref[table] == 1), -1e30, 0.0).astype(jnp.float32)
    right_bias = jnp.where((b == nblocks - 1) & (code_ref[table + 1] == 1), -1e30, 0.0).astype(jnp.float32)
    for h in range(width // HD):
        cols = slice(h * HD, (h + 1) * HD)
        vec = vec_ref[:, cols]
        prod = attend_tile(
            q_ref[:, cols], vec.astype(jnp.bfloat16), kvbuf[slot, 0, :, cols], kvbuf[slot, 1, :, cols],
            left_bias, right_bias,
        )
        out_ref[:, cols] = prod
        s = jnp.sum(vec * vec, axis=0, keepdims=True)
        c = jnp.sum(vec * prod, axis=0, keepdims=True)
        a = jnp.where(s > 0, c / jnp.where(s > 0, s, 1.0), 0.0)
        d = prod - a * vec
        acc[b, 0:1, cols] = s
        acc[b, 1:2, cols] = c
        acc[b, 2:3, cols] = jnp.sum(d * d, axis=0, keepdims=True)

    @pl.when(b == nblocks - 1)
    def _():
        s, c, r = combine(acc[:, 0, :], acc[:, 1, :], acc[:, 2, :])
        lane = lax.broadcasted_iota(jnp.int32, stat_ref.shape, 1) - 3 * chunk[1]
        stat_ref[...] = jnp.where(lane == 0, s, jnp.where(lane == 1, c, jnp.where(lane == 2, r, 0.0)))


def run_copies(plan, sems):
    copies = [pltpu.make_async_copy(src, dst, sems.at[i]) for i, (src, dst) in enumerate(plan)]
    for cp in copies:
        cp.start()
    for cp in copies:
        cp.wait()


def near_kernel(pick_ref, own, l1, r1, l2, r2, plus, minus, yp, y2, ym, sems):
    plan = []
    for i in range(6):
        plan.append((l2.at[pick_ref[i]], plus.at[i]))
        plan.append((r2.at[pick_ref[6 + i]], minus.at[i]))
    for row, out in enumerate((yp, y2, ym)):
        for i, src in enumerate((own, l1, r1, l2, r2)):
            plan.append((src.at[pick_ref[12 + row * 5 + i]], out.at[i]))
    plan.append((l1.at[l1.shape[0] - 1], yp.at[5]))
    plan.append((r1.at[0], ym.at[5]))
    run_copies(plan, sems)


def first_kernel(pick_ref, own, l1, r1, yp, y2, ym, sems):
    plan = []
    for row, out in enumerate((yp, y2, ym)):
        for i, src in enumerate((own, l1, r1)):
            plan.append((src.at[pick_ref[12 + row * 5 + i]], out.at[i]))
    plan.append((l1.at[l1.shape[0] - 1], yp.at[3]))
    plan.append((r1.at[0], ym.at[3]))
    run_copies(plan, sems)


def third_kernel(pick_ref, l2, r2, plus, minus, sems):
    plan = []
    for i in range(6):
        plan.append((l2.at[pick_ref[i]], plus.at[i]))
        plan.append((r2.at[pick_ref[6 + i]], minus.at[i]))
    run_copies(plan, sems)


def late_kernel(pick_ref, a3, b3, a4, b4, *refs):
    second = refs[:-4]
    outs, sems = refs[-4:-1], refs[-1]
    last = (a4.at[1], b4.at[0], b4.at[1])
    plan = []
    for row, out in enumerate(outs):
        plan += [(a3.at[row + 1], out.at[0]), (b3.at[row + 1], out.at[1]), (last[row], out.at[2])]
        for i, src in enumerate(second):
            plan.append((src.at[pick_ref[12 + row * 5 + 3 + i]], out.at[3 + i]))
    run_copies(plan, sems)


def split_kernel(pick_ref, blocks, p0, p1, p2, p3, sems):
    plan = []
    for i, out in enumerate((p0, p1, p2, p3)):
        rows = pl.ds(pl.multiple_of(pick_ref[29 + i], BS // NY), BS // NY)
        for g in range(2):
            plan.append((blocks.at[:, pick_ref[27 + g], rows], out.at[g]))
    run_copies(plan, sems)


def choose_kernel(at, pick_ref, *refs):
    srcs, out, sems = refs[:-2], refs[-2], refs[-1]
    for g in range(2):
        for k, src in enumerate(srcs):
            @pl.when(pick_ref[at + g] == k)
            def _(src=src, g=g):
                pltpu.make_async_copy(src.at[g], out.at[g], sems.at[g]).start()
    for g in range(2):
        pltpu.make_async_copy(srcs[0].at[g], out.at[g], sems.at[g]).wait()


def total(x):
    return jnp.sum(jnp.sum(x, axis=0, keepdims=True), axis=1, keepdims=True)


def combine(s, c, r):
    s_all = total(s)
    c_all = total(c)
    a = jnp.where(s > 0, c / jnp.where(s > 0, s, 1.0), 0.0)
    a_all = jnp.where(s_all > 0, c_all / jnp.where(s_all > 0, s_all, 1.0), 0.0)
    gap = a - a_all
    return s_all, c_all, total(r + (s * gap) * gap)


def finish_kernel(count, gathered, *refs):
    prods = refs[:CALLS]
    vec_ref, out_ref, coef_ref, ab = refs[CALLS:]
    step = pl.program_id(0)

    @pl.when(step == 0)
    def _():
        table = gathered[...]
        parts = [[table[:, 3 * k + i : 3 * k + i + 1] for i in range(3)] for k in range(CALLS)]
        alpha = sum(total(c) for _, c, _ in parts) * (1.0 / count)
        square = 0.0
        for s, c, r in parts:
            gap = jnp.where(s > 0, c / jnp.where(s > 0, s, 1.0), 0.0) - alpha
            square = square + total(r + (s * gap) * gap)
        beta = jnp.sqrt(square * (1.0 / count) + 1e-06)
        ab[0:1, :] = jnp.broadcast_to(alpha, (1, 128))
        ab[1:2, :] = jnp.broadcast_to(1.0 / beta, (1, 128))
        lane = lax.broadcasted_iota(jnp.int32, coef_ref.shape, 1)
        coef_ref[...] = jnp.where(lane == 0, alpha, beta)

    alpha = ab[0:1, 0:1]
    inv = ab[1:2, 0:1]
    for (first, heads), prod in zip(CHUNKS, prods):
        cols = slice(first * HD, (first + heads) * HD)
        out_ref[:, cols] = (prod[...] - alpha * vec_ref[:, cols]) * inv


def z_shift(d):
    return [(y * NZ + z, y * NZ + (z + d) % NZ) for y in range(NY) for z in range(NZ)]


def y_shift(d):
    return [(y * NZ + z, (y + d) % NY * NZ + z) for y in range(NY) for z in range(NZ)]


def send(x, pairs):
    return lax.ppermute(x, "ctx", pairs)


ANY = pl.BlockSpec(memory_space=pltpu.HBM)


def pack(kernel, picks, arrays, shapes, ncopies):
    return pl.pallas_call(
        kernel,
        out_shape=tuple(jax.ShapeDtypeStruct(shape, jnp.bfloat16) for shape in shapes),
        grid_spec=pltpu.PrefetchScalarGridSpec(
            num_scalar_prefetch=1,
            grid=(),
            in_specs=[ANY] * len(arrays),
            out_specs=tuple(pl.BlockSpec(memory_space=pltpu.VMEM) for _ in shapes),
            scratch_shapes=[pltpu.SemaphoreType.DMA((ncopies,))],
        ),
        cost_estimate=pl.CostEstimate(flops=0, bytes_accessed=6000000, transcendentals=0),
    )(picks, *arrays)


def tables(rand_blocks, global_ids, me, nblocks, nctx):
    my_y, my_z = me // NZ, me % NZ
    requests = rand_blocks.reshape(nctx, nblocks * 3)
    mine = lax.dynamic_index_in_dim(requests, me, 0, keepdims=False)
    pairs = [(i, 1, -2) for i in range(4)] + [(0, 2, -2), (1, 2, -2)]
    pairs += [(i, -1, 2) for i in range(4)] + [(2, -2, 2), (3, -2, 2)]
    for row in (1, 2, 3):
        pairs += [(row, 0, d) for d in (0, -1, 1, -2, 2)]
    offsets = jnp.array(pairs, jnp.int32)
    consumer = ((my_y + offsets[:, 0]) & (NY - 1)) * NZ + ((my_z + offsets[:, 1]) & (NZ - 1))
    source = my_y * NZ + ((my_z + offsets[:, 2]) & (NZ - 1))
    shift = nblocks.bit_length() - 1
    wanted = requests[consumer]
    picks = jnp.sum(
        jnp.where((wanted >> shift) == source[:, None], wanted & (nblocks - 1), 0), axis=1
    )
    g_shard = global_ids >> shift
    g_y, g_z = g_shard >> 3, g_shard & (NZ - 1)
    arange4 = jnp.arange(NY)
    picks = jnp.concatenate(
        [
            picks,
            global_ids & (nblocks - 1),
            ((my_y + arange4) & (NY - 1)) * (BS // NY),
            (my_y - g_y) & (NY - 1),
            (my_z - g_z) & (NZ - 1),
        ]
    ).astype(jnp.int32)
    src = mine >> shift
    inside = mine & (nblocks - 1)
    dy = ((src >> 3) - my_y) & (NY - 1)
    dz = (my_z - src) & (NZ - 1)
    late = (dz >= 3) & (dz <= 5)
    near_slot = jnp.where(late, 0, inside)
    order = jnp.where(
        late, jnp.where(dz == 3, 0, jnp.where(dz == 5, 1, 2)),
        jnp.where(dz == 0, 0, jnp.where(dz == 1, 1, jnp.where(dz == 7, 2, jnp.where(dz == 2, 3, 4)))),
    )
    row = jnp.where(dy == 1, 1, jnp.where(dy == 2, 2, 0))
    second = (dz == 2) | (dz == 6)
    block = jnp.arange(nblocks)
    edges = jnp.stack([me == 0, me == nctx - 1]).astype(jnp.int32)
    piece_rows = ((my_y - arange4) & (NY - 1)) * (BS // NY)
    codes = []
    for chunk, edge_slot in ((0, 5), (1, 3)):
        far = YP + row + jnp.where(late, LYP - YP, 0)
        if chunk:
            far = jnp.where(second, MP + row, far)
        rand_code = jnp.where(dy == 0, dz * 8 + near_slot, far * 8 + order).reshape(nblocks, 3)
        left = jnp.where(
            block == 0, jnp.where(my_z == 0, YP * 8 + edge_slot, L1 * 8 + nblocks - 1), block - 1
        )
        right = jnp.where(
            block == nblocks - 1, jnp.where(my_z == NZ - 1, YM * 8 + edge_slot, R1 * 8), block + 1
        )
        listed = jnp.concatenate([jnp.stack([left, block, right], axis=1), rand_code], axis=1)
        codes.append(jnp.concatenate([listed.reshape(-1), edges, piece_rows]).astype(jnp.int32))
    return picks, codes


def whole_step(queries, key_value, lanczos_vec, rand_blocks, global_ids):
    rows, width = queries.shape
    nblocks = rows // BS
    nctx = lax.axis_size("ctx")
    nhead = lax.axis_size("head")
    me = lax.axis_index("ctx")
    picks, codes = tables(rand_blocks, global_ids, me, nblocks, nctx)
    blocks = key_value.reshape(2, nblocks, BS, width)
    piece = (2, 2, BS // NY, width)
    quarters = pack(split_kernel, picks, (blocks,), (piece,) * NY, 8)
    held = (
        quarters[0],
        send(quarters[1], y_shift(1)),
        send(quarters[2], y_shift(2)),
        send(quarters[3], y_shift(-1)),
    )
    (mine,) = pack(functools.partial(choose_kernel, 33), picks, held, (piece,), 2)
    from_left = send(mine, z_shift(1))
    from_right = send(mine, z_shift(-1))
    (close,) = pack(
        functools.partial(choose_kernel, 35), picks,
        (mine, from_left, mine, mine, mine, mine, mine, from_right), (piece,), 2,
    )
    hop_left = send(close, z_shift(3))
    hop_right = send(close, z_shift(-3))
    (quarter,) = pack(
        functools.partial(choose_kernel, 35), picks,
        (close, close, hop_left, hop_left, hop_left, hop_right, hop_right, close), (piece,), 2,
    )
    pieces = (
        quarter, send(quarter, y_shift(1)), send(quarter, y_shift(2)), send(quarter, y_shift(-1))
    )
    cw = CHUNKS[0][1] * HD

    def slots(count):
        return (count, 2, BS, cw)

    def rows_of(packed):
        return tuple(send(x, y_shift(d)) for x, d in zip(packed, (1, 2, -1)))

    own, l1, r1, l2, r2 = [], [], [], [], []
    for k, (first, heads) in enumerate(CHUNKS):
        own.append(jnp.swapaxes(blocks[..., first * HD : (first + heads) * HD], 0, 1))
        l1.append(send(own[k], z_shift(1)))
        r1.append(send(own[k], z_shift(-1)))
        l2.append(send(l1[k], z_shift(1)))
        r2.append(send(r1[k], z_shift(-1)))
    plus, minus, *early = pack(
        near_kernel, picks, (own[0], l1[0], r1[0], l2[0], r2[0]),
        (slots(6), slots(6), slots(6), slots(5), slots(6)), 29,
    )
    y0 = rows_of(early)
    a3, b3 = send(plus, z_shift(1)), send(minus, z_shift(-1))
    a4, b4 = send(a3[4:6], z_shift(1)), send(b3[4:6], z_shift(-1))
    early = pack(first_kernel, picks, (own[1], l1[1], r1[1]), (slots(4), slots(3), slots(4)), 11)
    y1 = rows_of(early)
    plus, minus = pack(third_kernel, picks, (l2[1], r2[1]), (slots(6), slots(6)), 12)
    mid = rows_of(pack(late_kernel, picks, (a3, b3, a4, b4, l2[1], r2[1]), (slots(5),) * 3, 15))
    c3, d3 = send(plus, z_shift(1)), send(minus, z_shift(-1))
    c4, d4 = send(c3[4:6], z_shift(1)), send(d3[4:6], z_shift(-1))
    last = rows_of(pack(late_kernel, picks, (c3, d3, c4, d4), (slots(3),) * 3, 9))

    def by_code(y):
        return (y[0], y[2], y[1])

    sources = (
        (own[0], l1[0], l2[0], a3, a4, b3, r2[0], r1[0]) + by_code(y0) + by_code(mid),
        (own[1], l1[1], l2[1], c3, c4, d3, r2[1], r1[1]) + by_code(y1) + by_code(last) + by_code(mid),
    )
    products = []
    stats = []
    keys = LIST * BS
    for k, arrays in enumerate(sources):
        product, stat = pl.pallas_call(
            functools.partial(attention_kernel, nblocks, (CHUNKS[k][0], k), len(arrays)),
            out_shape=(
                jax.ShapeDtypeStruct((rows, cw), jnp.float32),
                jax.ShapeDtypeStruct((8, 128), jnp.float32),
            ),
            grid_spec=pltpu.PrefetchScalarGridSpec(
                num_scalar_prefetch=1,
                grid=(nblocks,),
                in_specs=[pl.BlockSpec((BS, cw), lambda b, *_, k=k: (b, k))] * 2
                + [ANY] * (len(arrays) + NY),
                out_specs=(
                    pl.BlockSpec((BS, cw), lambda b, *_: (b, 0)),
                    pl.BlockSpec((8, 128), lambda b, *_: (0, 0)),
                ),
                scratch_shapes=[
                    pltpu.VMEM((2, 2, keys, cw), jnp.bfloat16),
                    pltpu.SemaphoreType.DMA((2, 2 * LIST)),
                    pltpu.VMEM((nblocks, 8, cw), jnp.float32),
                ],
            ),
            cost_estimate=pl.CostEstimate(
                flops=10 * rows * keys * cw, bytes_accessed=16 * rows * cw,
                transcendentals=rows * keys * (cw // HD),
            ),
        )(codes[k], queries, lanczos_vec, *arrays, *pieces)
        products.append(product)
        stats.append(stat)
    sent = jnp.broadcast_to(sum(stats)[:1], (nctx * nhead, 128))
    gathered = lax.all_to_all(sent, ("ctx", "head"), 0, 0, tiled=True)
    count = float(rows * width * nctx * nhead)
    step = rows // 4
    fin_spec = pl.BlockSpec((step, width), lambda i: (i, 0))
    part_specs = [pl.BlockSpec((step, heads * HD), lambda i: (i, 0)) for _, heads in CHUNKS]
    next_vec, coef = pl.pallas_call(
        functools.partial(finish_kernel, count),
        out_shape=(
            jax.ShapeDtypeStruct((rows, width), jnp.float32),
            jax.ShapeDtypeStruct((8, 128), jnp.float32),
        ),
        grid=(4,),
        in_specs=[pl.BlockSpec((nctx * nhead, 128), lambda i: (0, 0))] + part_specs + [fin_spec],
        out_specs=(fin_spec, pl.BlockSpec((8, 128), lambda i: (0, 0))),
        scratch_shapes=[pltpu.VMEM((8, 128), jnp.float32)],
        name="finish",
    )(gathered, *products, lanczos_vec)
    return next_vec, coef[0, :2]


def solution(mesh):
    placed = (P("ctx", "head"), P(None, "ctx", "head"), P("ctx", "head"), P(), P())
    return jax.shard_map(
        whole_step, mesh=mesh, in_specs=placed, out_specs=(P("ctx", "head"), P()), check_vma=False
    )
```

profile of v0, /device:TPU:1, one launch (start us, length us, event | category | flops | bytes accessed | tf_op | source)
XLA Modules:
  0.0 318.2 jit_solution(13127307216886797963)
XLA Ops:
  5.0 4.0 %collective-permute-start.2 = (bf16[8,2,128,256]{3,2,1,0:T(8,128)(2,1)S(1)}, bf16[8,2,128,256]{3,2,1,0:T(8,128)(2,1)}, u32[]{:S(2)}, u32[]{:S(2)}) collective-permute-start(bf16[8,2,128,256]{3,2,1,0:T(8,128)(2,1)S(1)} %bitcast.23), channel_id=1, source_target_pairs={{0,56},{8,0},{16,8},{24,16},{32,24},{40,32},{48,40},{56,48},{64,12... | collective-permute-start | bytes 3145736 | tf_op jit(solution)/shard_map/ppermute | solution.py:260
  11.9 20.0 %collective-permute-done.l1.refs_1_ = bf16[8,2,128,256]{3,2,1,0:T(8,128)(2,1)} collective-permute-done((bf16[8,2,128,256]{3,2,1,0:T(8,128)(2,1)S(1)}, bf16[8,2,128,256]{3,2,1,0:T(8,128)(2,1)}, u32[]{:S(2)}, u32[]{:S(2)}) %collective-permute-start) | collective-permute-done | bytes 1048608 | tf_op jit(solution)/shard_map/ppermute | solution.py:260
  40.3 4.4 %collective-permute-done.18.refs_1_ = bf16[2,2,32,512]{3,2,1,0:T(8,128)(2,1)S(1)} collective-permute-done((bf16[2,2,32,512]{3,2,1,0:T(8,128)(2,1)}, bf16[2,2,32,512]{3,2,1,0:T(8,128)(2,1)S(1)}, u32[]{:S(2)}, u32[]{:S(2)}) %collective-permute-start.18) | collective-permute-done | bytes 131104 | tf_op jit(solution)/shard_map/ppermute | solution.py:260
  46.3 8.1 %collective-permute-done.11.l1.refs_1_ = bf16[8,2,128,256]{3,2,1,0:T(8,128)(2,1)} collective-permute-done((bf16[8,2,128,256]{3,2,1,0:T(8,128)(2,1)S(1)}, bf16[8,2,128,256]{3,2,1,0:T(8,128)(2,1)}, u32[]{:S(2)}, u32[]{:S(2)}) %collective-permute-start.11) | collective-permute-done | bytes 1048608 | tf_op jit(solution)/shard_map/ppermute | solution.py:260
  65.0 11.8 %collective-permute-done.1.l2.refs_2_ = bf16[8,2,128,256]{3,2,1,0:T(8,128)(2,1)} collective-permute-done((bf16[8,2,128,256]{3,2,1,0:T(8,128)(2,1)}, bf16[8,2,128,256]{3,2,1,0:T(8,128)(2,1)}, u32[]{:S(2)}, u32[]{:S(2)}) %collective-permute-start.1) | collective-permute-done | bytes 1048608 | tf_op jit(solution)/shard_map/ppermute | solution.py:260
  76.8 4.9 %shard_map.77 = (bf16[6,2,128,256]{3,2,1,0:T(8,128)(2,1)}, bf16[6,2,128,256]{3,2,1,0:T(8,128)(2,1)}, bf16[6,2,128,256]{3,2,1,0:T(8,128)(2,1)}, bf16[5,2,128,256]{3,2,1,0:T(8,128)(2,1)}, bf16[6,2,128,256]{3,2,1,0:T(8,128)(2,1)}) custom-call(s32[37]{0:T(128)} %concatenate.17.pick_ref, bf16[8,2,128,256]{3,2,1,0:T(8,128)(2,1)} %bitcast.24, ...), custom_call_target="tpu_custom_call" | custom-call | bytes 6000000 | tf_op jit(solution)/shard_map/pallas_call | solution.py:267
  84.5 17.5 %collective-permute-done.21.refs_1_ = bf16[2,2,32,512]{3,2,1,0:T(8,128)(2,1)S(1)} collective-permute-done((bf16[2,2,32,512]{3,2,1,0:T(8,128)(2,1)}, bf16[2,2,32,512]{3,2,1,0:T(8,128)(2,1)S(1)}, u32[]{:S(2)}, u32[]{:S(2)}) %collective-permute-start.21) | collective-permute-done | bytes 131104 | tf_op jit(solution)/shard_map/ppermute | solution.py:260
  103.2 14.7 %collective-permute-done.22.refs_7_ = bf16[2,2,32,512]{3,2,1,0:T(8,128)(2,1)S(1)} collective-permute-done((bf16[2,2,32,512]{3,2,1,0:T(8,128)(2,1)S(1)}, bf16[2,2,32,512]{3,2,1,0:T(8,128)(2,1)S(1)}, u32[]{:S(2)}, u32[]{:S(2)}) %collective-permute-start.22) | collective-permute-done | bytes 131104 | tf_op jit(solution)/shard_map/ppermute | solution.py:260
  120.8 4.8 %collective-permute-start.23 = (bf16[2,2,32,512]{3,2,1,0:T(8,128)(2,1)}, bf16[2,2,32,512]{3,2,1,0:T(8,128)(2,1)S(1)}, u32[]{:S(2)}, u32[]{:S(2)}) collective-permute-start(bf16[2,2,32,512]{3,2,1,0:T(8,128)(2,1)} %shard_map.81.refs_0_.refs_1_.refs_7_), channel_id=1, source_target_pairs={{0,24},{8,32},{16,40},{24,48},{32,56},{40,0},{48,8},{56,16},{64,88... | collective-permute-start | bytes 393224 | tf_op jit(solution)/shard_map/ppermute | solution.py:260
  125.6 4.5 %collective-permute-done.23.refs_2_.refs_3_.refs_4_ = bf16[2,2,32,512]{3,2,1,0:T(8,128)(2,1)S(1)} collective-permute-done((bf16[2,2,32,512]{3,2,1,0:T(8,128)(2,1)}, bf16[2,2,32,512]{3,2,1,0:T(8,128)(2,1)S(1)}, u32[]{:S(2)}, u32[]{:S(2)}) %collective-permute-start.23) | collective-permute-done | bytes 131104 | tf_op jit(solution)/shard_map/ppermute | solution.py:260
  130.2 6.4 %collective-permute-start.24 = (bf16[2,2,32,512]{3,2,1,0:T(8,128)(2,1)}, bf16[2,2,32,512]{3,2,1,0:T(8,128)(2,1)S(1)}, u32[]{:S(2)}, u32[]{:S(2)}) collective-permute-start(bf16[2,2,32,512]{3,2,1,0:T(8,128)(2,1)} %shard_map.81.refs_0_.refs_1_.refs_7_), channel_id=1, source_target_pairs={{0,40},{8,48},{16,56},{24,0},{32,8},{40,16},{48,24},{56,32},{64,10... | collective-permute-start | bytes 393224 | tf_op jit(solution)/shard_map/ppermute | solution.py:260
  153.0 4.0 %collective-permute-start.5 = (bf16[2,2,128,256]{3,2,1,0:T(8,128)(2,1)}, bf16[2,2,128,256]{3,2,1,0:T(8,128)(2,1)S(1)}, u32[]{:S(2)}, u32[]{:S(2)}) collective-permute-start(bf16[2,2,128,256]{3,2,1,0:T(8,128)(2,1)} %slice.50), channel_id=1, source_target_pairs={{0,8},{8,16},{16,24},{24,32},{32,40},{40,48},{48,56},{56,0},{64,72... | collective-permute-start | bytes 786440 | tf_op jit(solution)/shard_map/ppermute | solution.py:260
  159.6 3.4 %shard_map.84 = (bf16[6,2,128,256]{3,2,1,0:T(8,128)(2,1)}, bf16[6,2,128,256]{3,2,1,0:T(8,128)(2,1)}) custom-call(s32[37]{0:T(128)} %concatenate.17.pick_ref, bf16[8,2,128,256]{3,2,1,0:T(8,128)(2,1)} %copy-done, bf16[8,2,128,256]{3,2,1,0:T(8,128)(2,1)} %copy-done.1), custom_call_target="tpu_custom_call" | custom-call | bytes 6000000 | tf_op jit(solution)/shard_map/pallas_call | solution.py:267
  170.9 3.7 %shard_map.78 = (bf16[5,2,128,256]{3,2,1,0:T(8,128)(2,1)}, bf16[5,2,128,256]{3,2,1,0:T(8,128)(2,1)}, bf16[5,2,128,256]{3,2,1,0:T(8,128)(2,1)}) custom-call(s32[37]{0:T(128)} %concatenate.17.pick_ref, bf16[6,2,128,256]{3,2,1,0:T(8,128)(2,1)} %copy-done.5, bf16[6,2,128,256]{3,2,1,0:T(8,128)(2,1)} %collective-permute-done.6.b3.refs_5_, ...), custom_call_target="tpu_custom_call" | custom-call | bytes 6000000 | tf_op jit(solution)/shard_map/pallas_call | solution.py:267
  174.5 3.8 %collective-permute-done.9.refs_10_ = bf16[5,2,128,256]{3,2,1,0:T(8,128)(2,1)S(1)} collective-permute-done((bf16[5,2,128,256]{3,2,1,0:T(8,128)(2,1)}, bf16[5,2,128,256]{3,2,1,0:T(8,128)(2,1)S(1)}, u32[]{:S(2)}, u32[]{:S(2)}) %collective-permute-start.9) | collective-permute-done | bytes 655392 | tf_op jit(solution)/shard_map/ppermute | solution.py:260
  182.9 3.4 %collective-permute-start.17 = (bf16[5,2,128,256]{3,2,1,0:T(8,128)(2,1)}, bf16[5,2,128,256]{3,2,1,0:T(8,128)(2,1)}, u32[]{:S(2)}, u32[]{:S(2)}) collective-permute-start(bf16[5,2,128,256]{3,2,1,0:T(8,128)(2,1)} %get-tuple-element.35), channel_id=1, source_target_pairs={{0,128},{8,136},{16,144},{24,152},{32,160},{40,168},{48,176},{56,1... | collective-permute-start | bytes 1966088 | tf_op jit(solution)/shard_map/ppermute | solution.py:260
  187.8 11.7 %collective-permute-done.7.refs_8_ = bf16[6,2,128,256]{3,2,1,0:T(8,128)(2,1)} collective-permute-done((bf16[6,2,128,256]{3,2,1,0:T(8,128)(2,1)}, bf16[6,2,128,256]{3,2,1,0:T(8,128)(2,1)}, u32[]{:S(2)}, u32[]{:S(2)}) %collective-permute-start.7) | collective-permute-done | bytes 786464 | tf_op jit(solution)/shard_map/ppermute | solution.py:260
  200.2 7.8 %collective-permute-start.34 = (bf16[2,2,128,256]{3,2,1,0:T(8,128)(2,1)}, bf16[2,2,128,256]{3,2,1,0:T(8,128)(2,1)S(1)}, u32[]{:S(2)}, u32[]{:S(2)}) collective-permute-start(bf16[2,2,128,256]{3,2,1,0:T(8,128)(2,1)} %slice.54), channel_id=1, source_target_pairs={{0,56},{8,0},{16,8},{24,16},{32,24},{40,32},{48,40},{56,48},{64,12... | collective-permute-start | bytes 786440 | tf_op jit(solution)/shard_map/ppermute | solution.py:260
  208.2 3.8 %collective-permute-done.29.a4.refs_4_ = bf16[2,2,128,256]{3,2,1,0:T(8,128)(2,1)S(1)} collective-permute-done((bf16[2,2,128,256]{3,2,1,0:T(8,128)(2,1)}, bf16[2,2,128,256]{3,2,1,0:T(8,128)(2,1)S(1)}, u32[]{:S(2)}, u32[]{:S(2)}) %collective-permute-start.29) | collective-permute-done | bytes 262176 | tf_op jit(solution)/shard_map/ppermute | solution.py:260
  223.6 22.6 %shard_map.83 = (f32[1024,256]{1,0:T(8,128)}, f32[8,128]{1,0:T(8,128)}) custom-call(s32[54]{0:T(128)} %get-tuple-element.63.code_ref, bf16[1024,512]{1,0:T(8,128)(2,1)} %q_ref.3, f32[1024,512]{1,0:T(8,128)} %refs_2_.1, bf16[8,2,128,256]{3,2,1,0:T(8,128)(2,1)} %bitcast.25, bf16[8,2,128,256]{3,2,1,0:T(8,128)(2,1)} %collective-permute-done.l1.refs_1_, ...), custom_call_target="tpu_custom_call" | custom-call | flops 2684354560 | bytes 4194304 | tf_op jit(solution)/shard_map/pallas_call | solution.py:414
  246.2 5.1 %collective-permute-done.35.refs_11_ = bf16[3,2,128,256]{3,2,1,0:T(8,128)(2,1)S(1)} collective-permute-done((bf16[3,2,128,256]{3,2,1,0:T(8,128)(2,1)}, bf16[3,2,128,256]{3,2,1,0:T(8,128)(2,1)S(1)}, u32[]{:S(2)}, u32[]{:S(2)}) %collective-permute-start.35) | collective-permute-done | bytes 393248 | tf_op jit(solution)/shard_map/ppermute | solution.py:260
  252.4 22.8 %shard_map.87 = (f32[1024,256]{1,0:T(8,128)}, f32[8,128]{1,0:T(8,128)}) custom-call(s32[54]{0:T(128)} %get-tuple-element.62.code_ref, bf16[1024,512]{1,0:T(8,128)(2,1)} %q_ref.3, f32[1024,512]{1,0:T(8,128)} %refs_2_.1, bf16[8,2,128,256]{3,2,1,0:T(8,128)(2,1)} %bitcast.21, bf16[8,2,128,256]{3,2,1,0:T(8,128)(2,1)} %collective-permute-done.11.l1.refs_1_, ...), custom_call_target="tpu_custom_call" | custom-call | flops 2684354560 | bytes 4194304 | tf_op jit(solution)/shard_map/pallas_call | solution.py:414
  276.0 36.2 %all_to_all.8 = f32[256,1,128]{2,1,0:T(1,128)} all-to-all(f32[256,1,128]{2,1,0:T(1,128)S(1)} %broadcast_in_dim.52), channel_id=1, replica_groups=mesh['ctx'=32,'head'=8] {'ctx','head'}, dimensions={0} | all-to-all | bytes 262144 | tf_op jit(solution)/shard_map/all_to_all | solution.py:443
  312.1 4.9 %finish.1 = (f32[1024,512]{1,0:T(8,128)}, f32[8,128]{1,0:T(8,128)}) custom-call(f32[256,128]{1,0:T(8,128)} %bitcast.28, f32[1024,256]{1,0:T(8,128)} %get-tuple-element.50.refs_0_, f32[1024,256]{1,0:T(8,128)} %get-tuple-element.51.refs_1_, f32[1024,512]{1,0:T(8,128)} %refs_2_.1), custom_call_target="tpu_custom_call" | custom-call | tf_op jit(solution)/shard_map/finish/pallas_call | solution.py:448
  (164 shorter events, 82.7 us)
Async XLA Ops:
  2.5 29.4 %collective-permute-start = (bf16[8,2,128,256]{3,2,1,0:T(8,128)(2,1)S(1)}, bf16[8,2,128,256]{3,2,1,0:T(8,128)(2,1)}, u32[]{:S(2)}, u32[]{:S(2)}) collective-permute-start(bf16[8,2,128,256]{3,2,1,0:T(8,128)(2,1)S(1)} %bitcast.22), channel_id=1, source_target_pairs={{0,8},{8,16},{16,24},{24,32},{32,40},{40,48},{48,56},{56,0},{64,72... | collective-permute-start | bytes 3145736 | tf_op jit(solution)/shard_map/ppermute | solution.py:260
  5.0 26.9 %collective-permute-start.2 = (bf16[8,2,128,256]{3,2,1,0:T(8,128)(2,1)S(1)}, bf16[8,2,128,256]{3,2,1,0:T(8,128)(2,1)}, u32[]{:S(2)}, u32[]{:S(2)}) collective-permute-start(bf16[8,2,128,256]{3,2,1,0:T(8,128)(2,1)S(1)} %bitcast.23), channel_id=1, source_target_pairs={{0,56},{8,0},{16,8},{24,16},{32,24},{40,32},{48,40},{56,48},{64,12... | collective-permute-start | bytes 3145736 | tf_op jit(solution)/shard_map/ppermute | solution.py:260
  9.1 45.3 %collective-permute-start.11 = (bf16[8,2,128,256]{3,2,1,0:T(8,128)(2,1)S(1)}, bf16[8,2,128,256]{3,2,1,0:T(8,128)(2,1)}, u32[]{:S(2)}, u32[]{:S(2)}) collective-permute-start(bf16[8,2,128,256]{3,2,1,0:T(8,128)(2,1)S(1)} %bitcast.18), channel_id=1, source_target_pairs={{0,8},{8,16},{16,24},{24,32},{32,40},{40,48},{48,56},{56,0},{64,72... | collective-permute-start | bytes 3145736 | tf_op jit(solution)/shard_map/ppermute | solution.py:260
  9.2 45.2 %collective-permute-start.13 = (bf16[8,2,128,256]{3,2,1,0:T(8,128)(2,1)S(1)}, bf16[8,2,128,256]{3,2,1,0:T(8,128)(2,1)}, u32[]{:S(2)}, u32[]{:S(2)}) collective-permute-start(bf16[8,2,128,256]{3,2,1,0:T(8,128)(2,1)S(1)} %bitcast.19), channel_id=1, source_target_pairs={{0,56},{8,0},{16,8},{24,16},{32,24},{40,32},{48,40},{56,48},{64,12... | collective-permute-start | bytes 3145736 | tf_op jit(solution)/shard_map/ppermute | solution.py:260
  31.9 44.9 %collective-permute-start.1 = (bf16[8,2,128,256]{3,2,1,0:T(8,128)(2,1)}, bf16[8,2,128,256]{3,2,1,0:T(8,128)(2,1)}, u32[]{:S(2)}, u32[]{:S(2)}) collective-permute-start(bf16[8,2,128,256]{3,2,1,0:T(8,128)(2,1)} %collective-permute-done.l1.refs_1_), channel_id=1, source_target_pairs={{0,8},{8,16},{16,24},{24,32},{32,40},{40,48},{48,56},{56,0},{64,72... | collective-permute-start | bytes 3145736 | tf_op jit(solution)/shard_map/ppermute | solution.py:260
  31.9 44.9 %collective-permute-start.3 = (bf16[8,2,128,256]{3,2,1,0:T(8,128)(2,1)}, bf16[8,2,128,256]{3,2,1,0:T(8,128)(2,1)}, u32[]{:S(2)}, u32[]{:S(2)}) collective-permute-start(bf16[8,2,128,256]{3,2,1,0:T(8,128)(2,1)} %collective-permute-done.2.r1.refs_7_), channel_id=1, source_target_pairs={{0,56},{8,0},{16,8},{24,16},{32,24},{40,32},{48,40},{56,48},{64,12... | collective-permute-start | bytes 3145736 | tf_op jit(solution)/shard_map/ppermute | solution.py:260
  54.4 95.4 %collective-permute-start.12 = (bf16[8,2,128,256]{3,2,1,0:T(8,128)(2,1)}, bf16[8,2,128,256]{3,2,1,0:T(8,128)(2,1)S(1)}, u32[]{:S(2)}, u32[]{:S(2)}) collective-permute-start(bf16[8,2,128,256]{3,2,1,0:T(8,128)(2,1)} %collective-permute-done.11.l1.refs_1_), channel_id=1, source_target_pairs={{0,8},{8,16},{16,24},{24,32},{32,40},{40,48},{48,56},{56,0},{64,72... | collective-permute-start | bytes 3145736 | tf_op jit(solution)/shard_map/ppermute | solution.py:260
  54.4 104.3 %collective-permute-start.14 = (bf16[8,2,128,256]{3,2,1,0:T(8,128)(2,1)}, bf16[8,2,128,256]{3,2,1,0:T(8,128)(2,1)S(1)}, u32[]{:S(2)}, u32[]{:S(2)}) collective-permute-start(bf16[8,2,128,256]{3,2,1,0:T(8,128)(2,1)} %collective-permute-done.13.r1.refs_7_), channel_id=1, source_target_pairs={{0,56},{8,0},{16,8},{24,16},{32,24},{40,32},{48,40},{56,48},{64,12... | collective-permute-start | bytes 3145736 | tf_op jit(solution)/shard_map/ppermute | solution.py:260
  64.9 37.1 %collective-permute-start.21 = (bf16[2,2,32,512]{3,2,1,0:T(8,128)(2,1)}, bf16[2,2,32,512]{3,2,1,0:T(8,128)(2,1)S(1)}, u32[]{:S(2)}, u32[]{:S(2)}) collective-permute-start(bf16[2,2,32,512]{3,2,1,0:T(8,128)(2,1)} %shard_map.80.refs_0_.refs_2_.refs_3_.refs_4_.refs_5_.refs_6_), channel_id=1, source_target_pairs={{0,8},{8,16},{16,24},{24,32},{32,40},{40,48},{48,56},{56,0},{64,72... | collective-permute-start | bytes 393224 | tf_op jit(solution)/shard_map/ppermute | solution.py:260
  81.8 69.0 %collective-permute-start.4 = (bf16[6,2,128,256]{3,2,1,0:T(8,128)(2,1)}, bf16[6,2,128,256]{3,2,1,0:T(8,128)(2,1)S(1)}, u32[]{:S(2)}, u32[]{:S(2)}) collective-permute-start(bf16[6,2,128,256]{3,2,1,0:T(8,128)(2,1)} %get-tuple-element.28), channel_id=1, source_target_pairs={{0,8},{8,16},{16,24},{24,32},{32,40},{40,48},{48,56},{56,0},{64,72... | collective-permute-start | bytes 2359304 | tf_op jit(solution)/shard_map/ppermute | solution.py:260
  81.9 71.1 %collective-permute-start.6 = (bf16[6,2,128,256]{3,2,1,0:T(8,128)(2,1)}, bf16[6,2,128,256]{3,2,1,0:T(8,128)(2,1)}, u32[]{:S(2)}, u32[]{:S(2)}) collective-permute-start(bf16[6,2,128,256]{3,2,1,0:T(8,128)(2,1)} %get-tuple-element.29), channel_id=1, source_target_pairs={{0,56},{8,0},{16,8},{24,16},{32,24},{40,32},{48,40},{56,48},{64,12... | collective-permute-start | bytes 2359304 | tf_op jit(solution)/shard_map/ppermute | solution.py:260
  147.7 19.4 %collective-permute-start.33 = (bf16[3,2,128,256]{3,2,1,0:T(8,128)(2,1)}, bf16[3,2,128,256]{3,2,1,0:T(8,128)(2,1)}, u32[]{:S(2)}, u32[]{:S(2)}) collective-permute-start(bf16[3,2,128,256]{3,2,1,0:T(8,128)(2,1)} %get-tuple-element.45), channel_id=1, source_target_pairs={{0,128},{8,136},{16,144},{24,152},{32,160},{40,168},{48,176},{56,1... | collective-permute-start | bytes 1179656 | tf_op jit(solution)/shard_map/ppermute | solution.py:260
  163.7 17.4 %collective-permute-start.28 = (bf16[6,2,128,256]{3,2,1,0:T(8,128)(2,1)}, bf16[6,2,128,256]{3,2,1,0:T(8,128)(2,1)S(1)}, u32[]{:S(2)}, u32[]{:S(2)}) collective-permute-start(bf16[6,2,128,256]{3,2,1,0:T(8,128)(2,1)} %get-tuple-element.41), channel_id=1, source_target_pairs={{0,8},{8,16},{16,24},{24,32},{32,40},{40,48},{48,56},{56,0},{64,72... | collective-permute-start | bytes 2359304 | tf_op jit(solution)/shard_map/ppermute | solution.py:260
  164.4 18.5 %collective-permute-start.30 = (bf16[6,2,128,256]{3,2,1,0:T(8,128)(2,1)}, bf16[6,2,128,256]{3,2,1,0:T(8,128)(2,1)S(1)}, u32[]{:S(2)}, u32[]{:S(2)}) collective-permute-start(bf16[6,2,128,256]{3,2,1,0:T(8,128)(2,1)} %get-tuple-element.42), channel_id=1, source_target_pairs={{0,56},{8,0},{16,8},{24,16},{32,24},{40,32},{48,40},{56,48},{64,12... | collective-permute-start | bytes 2359304 | tf_op jit(solution)/shard_map/ppermute | solution.py:260
  168.2 31.3 %collective-permute-start.7 = (bf16[6,2,128,256]{3,2,1,0:T(8,128)(2,1)}, bf16[6,2,128,256]{3,2,1,0:T(8,128)(2,1)}, u32[]{:S(2)}, u32[]{:S(2)}) collective-permute-start(bf16[6,2,128,256]{3,2,1,0:T(8,128)(2,1)} %get-tuple-element.30), channel_id=1, source_target_pairs={{0,64},{8,72},{16,80},{24,88},{32,96},{40,104},{48,112},{56,120},{... | collective-permute-start | bytes 2359304 | tf_op jit(solution)/shard_map/ppermute | solution.py:260
  168.6 31.6 %collective-permute-start.8 = (bf16[6,2,128,256]{3,2,1,0:T(8,128)(2,1)}, bf16[6,2,128,256]{3,2,1,0:T(8,128)(2,1)}, u32[]{:S(2)}, u32[]{:S(2)}) collective-permute-start(bf16[6,2,128,256]{3,2,1,0:T(8,128)(2,1)} %get-tuple-element.31), channel_id=1, source_target_pairs={{0,192},{8,200},{16,208},{24,216},{32,224},{40,232},{48,240},{56,2... | collective-permute-start | bytes 2359304 | tf_op jit(solution)/shard_map/ppermute | solution.py:260
  178.4 40.6 %collective-permute-start.15 = (bf16[5,2,128,256]{3,2,1,0:T(8,128)(2,1)}, bf16[5,2,128,256]{3,2,1,0:T(8,128)(2,1)S(1)}, u32[]{:S(2)}, u32[]{:S(2)}) collective-permute-start(bf16[5,2,128,256]{3,2,1,0:T(8,128)(2,1)} %get-tuple-element.33), channel_id=1, source_target_pairs={{0,64},{8,72},{16,80},{24,88},{32,96},{40,104},{48,112},{56,120},{... | collective-permute-start | bytes 1966088 | tf_op jit(solution)/shard_map/ppermute | solution.py:260
  181.1 37.8 %collective-permute-start.16 = (bf16[5,2,128,256]{3,2,1,0:T(8,128)(2,1)}, bf16[5,2,128,256]{3,2,1,0:T(8,128)(2,1)S(1)}, u32[]{:S(2)}, u32[]{:S(2)}) collective-permute-start(bf16[5,2,128,256]{3,2,1,0:T(8,128)(2,1)} %get-tuple-element.34), channel_id=1, source_target_pairs={{0,192},{8,200},{16,208},{24,216},{32,224},{40,232},{48,240},{56,2... | collective-permute-start | bytes 1966088 | tf_op jit(solution)/shard_map/ppermute | solution.py:260
  182.9 38.9 %collective-permute-start.17 = (bf16[5,2,128,256]{3,2,1,0:T(8,128)(2,1)}, bf16[5,2,128,256]{3,2,1,0:T(8,128)(2,1)}, u32[]{:S(2)}, u32[]{:S(2)}) collective-permute-start(bf16[5,2,128,256]{3,2,1,0:T(8,128)(2,1)} %get-tuple-element.35), channel_id=1, source_target_pairs={{0,128},{8,136},{16,144},{24,152},{32,160},{40,168},{48,176},{56,1... | collective-permute-start | bytes 1966088 | tf_op jit(solution)/shard_map/ppermute | solution.py:260
  212.0 34.2 %collective-permute-start.31 = (bf16[4,2,128,256]{3,2,1,0:T(8,128)(2,1)}, bf16[4,2,128,256]{3,2,1,0:T(8,128)(2,1)}, u32[]{:S(2)}, u32[]{:S(2)}) collective-permute-start(bf16[4,2,128,256]{3,2,1,0:T(8,128)(2,1)} %get-tuple-element.43), channel_id=1, source_target_pairs={{0,64},{8,72},{16,80},{24,88},{32,96},{40,104},{48,112},{56,120},{... | collective-permute-start | bytes 1572872 | tf_op jit(solution)/shard_map/ppermute | solution.py:260
  212.0 34.2 %collective-permute-start.32 = (bf16[4,2,128,256]{3,2,1,0:T(8,128)(2,1)}, bf16[4,2,128,256]{3,2,1,0:T(8,128)(2,1)}, u32[]{:S(2)}, u32[]{:S(2)}) collective-permute-start(bf16[4,2,128,256]{3,2,1,0:T(8,128)(2,1)} %get-tuple-element.44), channel_id=1, source_target_pairs={{0,192},{8,200},{16,208},{24,216},{32,224},{40,232},{48,240},{56,2... | collective-permute-start | bytes 1572872 | tf_op jit(solution)/shard_map/ppermute | solution.py:260
  218.9 32.4 %collective-permute-start.35 = (bf16[3,2,128,256]{3,2,1,0:T(8,128)(2,1)}, bf16[3,2,128,256]{3,2,1,0:T(8,128)(2,1)S(1)}, u32[]{:S(2)}, u32[]{:S(2)}) collective-permute-start(bf16[3,2,128,256]{3,2,1,0:T(8,128)(2,1)} %get-tuple-element.46), channel_id=1, source_target_pairs={{0,64},{8,72},{16,80},{24,88},{32,96},{40,104},{48,112},{56,120},{... | collective-permute-start | bytes 1179656 | tf_op jit(solution)/shard_map/ppermute | solution.py:260
  218.9 32.4 %collective-permute-start.36 = (bf16[3,2,128,256]{3,2,1,0:T(8,128)(2,1)}, bf16[3,2,128,256]{3,2,1,0:T(8,128)(2,1)S(1)}, u32[]{:S(2)}, u32[]{:S(2)}) collective-permute-start(bf16[3,2,128,256]{3,2,1,0:T(8,128)(2,1)} %get-tuple-element.47), channel_id=1, source_target_pairs={{0,192},{8,200},{16,208},{24,216},{32,224},{40,232},{48,240},{56,2... | collective-permute-start | bytes 1179656 | tf_op jit(solution)/shard_map/ppermute | solution.py:260
  221.8 29.6 %collective-permute-start.37 = (bf16[3,2,128,256]{3,2,1,0:T(8,128)(2,1)}, bf16[3,2,128,256]{3,2,1,0:T(8,128)(2,1)S(1)}, u32[]{:S(2)}, u32[]{:S(2)}) collective-permute-start(bf16[3,2,128,256]{3,2,1,0:T(8,128)(2,1)} %get-tuple-element.48), channel_id=1, source_target_pairs={{0,128},{8,136},{16,144},{24,152},{32,160},{40,168},{48,176},{56,1... | collective-permute-start | bytes 1179656 | tf_op jit(solution)/shard_map/ppermute | solution.py:260
  (47 other events, 674.2 us)
where the time goes:
time: 319 us; the launch traced here: 318 us
  waiting for transfers between devices  116 us (36%)
  Pallas kernels  77.9 us (24%)
  starting transfers between devices  71.5 us (22%)
  blocking collectives  36.2 us (11%)
  local copies, waits for them, and re-layouts  13.3 us (4%)
    ppermute x38, waiting for transfers between devices, send(): return lax.ppermute(x, 'ctx', pairs)  116 us
    ppermute x38, starting transfers between devices, send(): return lax.ppermute(x, 'ctx', pairs)  71.5 us
    pallas_call x2, Pallas kernels, whole_step(): pl.pallas_call(functools.partial(attention_kernel, nblocks, (CHUNKS[k][0]...  45.4 us
    all_to_all x1, blocking collectives, whole_step(): gathered = lax.all_to_all(sent, ('ctx', 'head'), 0, 0, tiled=True)  36.2 us
    pallas_call x9, Pallas kernels, pack(): pl.pallas_call(kernel, out_shape=tuple((jax.ShapeDtypeStruct(shape, jnp.b...  27.6 us
  transfers between devices with their start and end apart: 38, of which 18 were waited for; matrix products, arithmetic and copies ran while one was open for 2% of the time, Pallas kernels for 16%

commit v1 on v0

--- a/solution.py
+++ b/solution.py
@@ -16,31 +16,44 @@
 NT = (((1,), (1,)), ((), ()))
 
 
-def attend_tile(q, tangent, keys, values, left_bias, right_bias):
-    both = jnp.concatenate([q, tangent], axis=0)
-    logits = lax.dot_general(both, keys, NT, preferred_element_type=jnp.float32)
-    scores = logits[:BS]
-    dots = logits[BS:]
-    scores = jnp.concatenate(
-        [
-            scores[:, :BS] + left_bias,
-            scores[:, BS : 2 * BS],
-            scores[:, 2 * BS : 3 * BS] + right_bias,
-            scores[:, 3 * BS :],
-        ],
-        axis=1,
-    )
-    row_top = jnp.max(scores, axis=1, keepdims=True)
-    weights = jnp.exp2((scores - row_top) * (SCALE * LOG2E))
-    inv_total = 1.0 / jnp.sum(weights, axis=1, keepdims=True)
-    prob = weights * inv_total
-    center = jnp.sum(prob * dots, axis=1, keepdims=True)
-    first = ((prob * SCALE) * (dots - center)).astype(jnp.bfloat16)
-    dout = jnp.dot(first, values, preferred_element_type=jnp.float32).astype(jnp.bfloat16)
-    dprob = lax.dot_general(dout, values, NT, preferred_element_type=jnp.float32)
-    center_two = jnp.sum(prob * dprob, axis=1, keepdims=True)
-    second = (prob * (dprob - center_two)).astype(jnp.bfloat16)
-    return jnp.dot(second, keys, preferred_element_type=jnp.float32) * SCALE
+def attend_tiles(tiles, left_bias, right_bias):
+    count = range(len(tiles))
+    logits = [
+        lax.dot_general(
+            jnp.concatenate([q, tangent], axis=0), keys, NT, preferred_element_type=jnp.float32
+        )
+        for q, tangent, keys, _ in tiles
+    ]
+    prob, dots = [], []
+    for x in logits:
+        scores = x[:BS]
+        scores = jnp.concatenate(
+            [
+                scores[:, :BS] + left_bias,
+                scores[:, BS : 2 * BS],
+                scores[:, 2 * BS : 3 * BS] + right_bias,
+                scores[:, 3 * BS :],
+            ],
+            axis=1,
+        )
+        row_top = jnp.max(scores, axis=1, keepdims=True)
+        weights = jnp.exp2((scores - row_top) * (SCALE * LOG2E))
+        prob.append(weights * (1.0 / jnp.sum(weights, axis=1, keepdims=True)))
+        dots.append(x[BS:])
+    dout = []
+    for i in count:
+        center = jnp.sum(prob[i] * dots[i], axis=1, keepdims=True)
+        first = ((prob[i] * SCALE) * (dots[i] - center)).astype(jnp.bfloat16)
+        dout.append(jnp.dot(first, tiles[i][3], preferred_element_type=jnp.float32).astype(jnp.bfloat16))
+    dprob = [
+        lax.dot_general(dout[i], tiles[i][3], NT, preferred_element_type=jnp.float32) for i in count
+    ]
+    out = []
+    for i in count:
+        center = jnp.sum(prob[i] * dprob[i], axis=1, keepdims=True)
+        second = (prob[i] * (dprob[i] - center)).astype(jnp.bfloat16)
+        out.append(jnp.dot(second, tiles[i][2], preferred_element_type=jnp.float32) * SCALE)
+    return out
 
 
 NY, NZ = 4, 8
@@ -114,13 +127,16 @@
 
     left_bias = jnp.where((b == 0) & (code_ref[table] == 1), -1e30, 0.0).astype(jnp.float32)
     right_bias = jnp.where((b == nblocks - 1) & (code_ref[table + 1] == 1), -1e30, 0.0).astype(jnp.float32)
-    for h in range(width // HD):
-        cols = slice(h * HD, (h + 1) * HD)
+    heads = [slice(h * HD, (h + 1) * HD) for h in range(width // HD)]
+    tiles = [
+        (
+            q_ref[:, cols], vec_ref[:, cols].astype(jnp.bfloat16),
+            kvbuf[slot, 0, :, cols], kvbuf[slot, 1, :, cols],
+        )
+        for cols in heads
+    ]
+    for cols, prod in zip(heads, attend_tiles(tiles, left_bias, right_bias)):
         vec = vec_ref[:, cols]
-        prod = attend_tile(
-            q_ref[:, cols], vec.astype(jnp.bfloat16), kvbuf[slot, 0, :, cols], kvbuf[slot, 1, :, cols],
-            left_bias, right_bias,
-        )
         out_ref[:, cols] = prod
         s = jnp.sum(vec * vec, axis=0, keepdims=True)
         c = jnp.sum(vec * prod, axis=0, keepdims=True)
@@ -145,46 +161,42 @@
         cp.wait()
 
 
-def near_kernel(pick_ref, own, l1, r1, l2, r2, plus, minus, yp, y2, ym, sems):
+def first_kernel(pick_ref, own_a, l1_a, r1_a, own_b, l1_b, r1_b, yp, y2, ym, sems):
+    plan = []
+    for k, arrays in enumerate(((own_a, l1_a, r1_a), (own_b, l1_b, r1_b))):
+        for row, (out, step) in enumerate(((yp, 4), (y2, 3), (ym, 4))):
+            for i, src in enumerate(arrays):
+                plan.append((src.at[pick_ref[12 + row * 5 + i]], out.at[k * step + i]))
+        plan.append((arrays[1].at[own_a.shape[0] - 1], yp.at[k * 4 + 3]))
+        plan.append((arrays[2].at[0], ym.at[k * 4 + 3]))
+    run_copies(plan, sems)
+
+
+def third_hop(pick_ref, l2, r2, plus, minus):
     plan = []
     for i in range(6):
         plan.append((l2.at[pick_ref[i]], plus.at[i]))
         plan.append((r2.at[pick_ref[6 + i]], minus.at[i]))
+    return plan
+
+
+def third_kernel(pick_ref, l2, r2, plus, minus, sems):
+    run_copies(third_hop(pick_ref, l2, r2, plus, minus), sems)
+
+
+def second_kernel(pick_ref, l2_a, r2_a, l2_b, r2_b, plus, minus, yp, y2, ym, sems):
+    plan = third_hop(pick_ref, l2_b, r2_b, plus, minus)
     for row, out in enumerate((yp, y2, ym)):
-        for i, src in enumerate((own, l1, r1, l2, r2)):
-            plan.append((src.at[pick_ref[12 + row * 5 + i]], out.at[i]))
-    plan.append((l1.at[l1.shape[0] - 1], yp.at[5]))
-    plan.append((r1.at[0], ym.at[5]))
+        for i, src in enumerate((l2_a, r2_a, l2_b, r2_b)):
+            plan.append((src.at[pick_ref[12 + row * 5 + 3 + i % 2]], out.at[i]))
     run_copies(plan, sems)
 
 
-def first_kernel(pick_ref, own, l1, r1, yp, y2, ym, sems):
+def late_kernel(a3, b3, a4, b4, yp, y2, ym, sems):
+    last = (a4.at[1], b4.at[0], b4.at[1])
     plan = []
     for row, out in enumerate((yp, y2, ym)):
-        for i, src in enumerate((own, l1, r1)):
-            plan.append((src.at[pick_ref[12 + row * 5 + i]], out.at[i]))
-    plan.append((l1.at[l1.shape[0] - 1], yp.at[3]))
-    plan.append((r1.at[0], ym.at[3]))
-    run_copies(plan, sems)
-
-
-def third_kernel(pick_ref, l2, r2, plus, minus, sems):
-    plan = []
-    for i in range(6):
-        plan.append((l2.at[pick_ref[i]], plus.at[i]))
-        plan.append((r2.at[pick_ref[6 + i]], minus.at[i]))
-    run_copies(plan, sems)
-
-
-def late_kernel(pick_ref, a3, b3, a4, b4, *refs):
-    second = refs[:-4]
-    outs, sems = refs[-4:-1], refs[-1]
-    last = (a4.at[1], b4.at[0], b4.at[1])
-    plan = []
-    for row, out in enumerate(outs):
         plan += [(a3.at[row + 1], out.at[0]), (b3.at[row + 1], out.at[1]), (last[row], out.at[2])]
-        for i, src in enumerate(second):
-            plan.append((src.at[pick_ref[12 + row * 5 + 3 + i]], out.at[3 + i]))
     run_copies(plan, sems)
 
 
@@ -264,18 +276,19 @@
 
 
 def pack(kernel, picks, arrays, shapes, ncopies):
+    scalars = () if picks is None else (picks,)
     return pl.pallas_call(
         kernel,
         out_shape=tuple(jax.ShapeDtypeStruct(shape, jnp.bfloat16) for shape in shapes),
         grid_spec=pltpu.PrefetchScalarGridSpec(
-            num_scalar_prefetch=1,
+            num_scalar_prefetch=len(scalars),
             grid=(),
             in_specs=[ANY] * len(arrays),
             out_specs=tuple(pl.BlockSpec(memory_space=pltpu.VMEM) for _ in shapes),
             scratch_shapes=[pltpu.SemaphoreType.DMA((ncopies,))],
         ),
         cost_estimate=pl.CostEstimate(flops=0, bytes_accessed=6000000, transcendentals=0),
-    )(picks, *arrays)
+    )(*scalars, *arrays)
 
 
 def tables(rand_blocks, global_ids, me, nblocks, nctx):
@@ -322,11 +335,11 @@
     edges = jnp.stack([me == 0, me == nctx - 1]).astype(jnp.int32)
     piece_rows = ((my_y - arange4) & (NY - 1)) * (BS // NY)
     codes = []
-    for chunk, edge_slot in ((0, 5), (1, 3)):
-        far = YP + row + jnp.where(late, LYP - YP, 0)
-        if chunk:
-            far = jnp.where(second, MP + row, far)
-        rand_code = jnp.where(dy == 0, dz * 8 + near_slot, far * 8 + order).reshape(nblocks, 3)
+    for chunk in range(2):
+        edge_slot = chunk * 4 + 3
+        far = jnp.where(late, LYP, jnp.where(second, MP, YP)) + row
+        base = jnp.where(late, 0, jnp.where(second, chunk * 2 - 3, chunk * jnp.where(row == 2, 3, 4)))
+        rand_code = jnp.where(dy == 0, dz * 8 + near_slot, far * 8 + order + base).reshape(nblocks, 3)
         left = jnp.where(
             block == 0, jnp.where(my_z == 0, YP * 8 + edge_slot, L1 * 8 + nblocks - 1), block - 1
         )
@@ -385,27 +398,31 @@
         r1.append(send(own[k], z_shift(-1)))
         l2.append(send(l1[k], z_shift(1)))
         r2.append(send(r1[k], z_shift(-1)))
-    plus, minus, *early = pack(
-        near_kernel, picks, (own[0], l1[0], r1[0], l2[0], r2[0]),
-        (slots(6), slots(6), slots(6), slots(5), slots(6)), 29,
-    )
-    y0 = rows_of(early)
+    y1 = rows_of(
+        pack(
+            first_kernel, picks, (own[0], l1[0], r1[0], own[1], l1[1], r1[1]),
+            (slots(8), slots(6), slots(8)), 22,
+        ),
+    )
+    plus, minus = pack(third_kernel, picks, (l2[0], r2[0]), (slots(6), slots(6)), 12)
     a3, b3 = send(plus, z_shift(1)), send(minus, z_shift(-1))
+    plus, minus, *two = pack(
+        second_kernel, picks, (l2[0], r2[0], l2[1], r2[1]),
+        (slots(6), slots(6)) + (slots(4),) * 3, 24,
+    )
+    y2 = rows_of(two)
+    c3, d3 = send(plus, z_shift(1)), send(minus, z_shift(-1))
     a4, b4 = send(a3[4:6], z_shift(1)), send(b3[4:6], z_shift(-1))
-    early = pack(first_kernel, picks, (own[1], l1[1], r1[1]), (slots(4), slots(3), slots(4)), 11)
-    y1 = rows_of(early)
-    plus, minus = pack(third_kernel, picks, (l2[1], r2[1]), (slots(6), slots(6)), 12)
-    mid = rows_of(pack(late_kernel, picks, (a3, b3, a4, b4, l2[1], r2[1]), (slots(5),) * 3, 15))
-    c3, d3 = send(plus, z_shift(1)), send(minus, z_shift(-1))
     c4, d4 = send(c3[4:6], z_shift(1)), send(d3[4:6], z_shift(-1))
-    last = rows_of(pack(late_kernel, picks, (c3, d3, c4, d4), (slots(3),) * 3, 9))
+    y3a = rows_of(pack(late_kernel, None, (a3, b3, a4, b4), (slots(3),) * 3, 9))
+    y3b = rows_of(pack(late_kernel, None, (c3, d3, c4, d4), (slots(3),) * 3, 9))
 
     def by_code(y):
         return (y[0], y[2], y[1])
 
     sources = (
-        (own[0], l1[0], l2[0], a3, a4, b3, r2[0], r1[0]) + by_code(y0) + by_code(mid),
-        (own[1], l1[1], l2[1], c3, c4, d3, r2[1], r1[1]) + by_code(y1) + by_code(last) + by_code(mid),
+        (own[0], l1[0], l2[0], a3, a4, b3, r2[0], r1[0]) + by_code(y1) + by_code(y3a) + by_code(y2),
+        (own[1], l1[1], l2[1], c3, c4, d3, r2[1], r1[1]) + by_code(y1) + by_code(y3b) + by_code(y2),
     )
     products = []
     stats = []

time: 319 us -> 313 us (0.981)
  Pallas kernels: 77.9 us -> 64.2 us
  local copies, waits for them, and re-layouts: 13.3 us -> 20.7 us
  starting transfers between devices: 71.5 us -> 68 us
    pallas_call x2, Pallas kernels: 45.4 us -> 33.1 us  [whole_step(): pl.pallas_call(functools.partial(attention_kernel, nblocks, (CHUNKS[k][0]...]
    select_n x2 -> x3, local copies, waits for them, and re-layouts: 0.15 us -> 3.9 us  [the longest x1 1.33 us: tables(): jnp.where(dz == 0, 0, jnp.where(dz == 1, 1, jnp.where(dz == 7, 2, jnp.whe...]
    ppermute x38, starting transfers between devices: 71.5 us -> 68 us  [send(): return lax.ppermute(x, 'ctx', pairs)]
  transfers between devices with their start and end apart: 38 -> 38, of which waited for: 18 -> 14; matrix products, arithmetic and copies ran while one was open for 2% -> 5% of each run, Pallas kernels for 16% -> 14%
where the time goes in v1:
time: 313 us; the launch traced here: 312 us
  waiting for transfers between devices  116 us (37%)
  starting transfers between devices  68 us (22%)
  Pallas kernels  64.2 us (21%)
  blocking collectives  37.2 us (12%)
  local copies, waits for them, and re-layouts  20.7 us (7%)
  other arithmetic  4.8 us (2%)
    ppermute x38, waiting for transfers between devices, send(): return lax.ppermute(x, 'ctx', pairs)  116 us
    ppermute x38, starting transfers between devices, send(): return lax.ppermute(x, 'ctx', pairs)  68 us
    all_to_all x1, blocking collectives, whole_step(): gathered = lax.all_to_all(sent, ('ctx', 'head'), 0, 0, tiled=True)  37.2 us
    pallas_call x2, Pallas kernels, whole_step(): pl.pallas_call(functools.partial(attention_kernel, nblocks, (CHUNKS[k][0]...  33.1 us
    pallas_call x9, Pallas kernels, pack(): pl.pallas_call(kernel, out_shape=tuple((jax.ShapeDtypeStruct(shape, jnp.b...  26.2 us
  transfers between devices with their start and end apart: 38, of which 14 were waited for; matrix products, arithmetic and copies ran while one was open for 5% of the time, Pallas kernels for 14%

profile of v1, /device:TPU:1, one launch (start us, length us, event | category | flops | bytes accessed | tf_op | source)
XLA Modules:
  0.0 312.2 jit_solution(1596651032093139773)
XLA Ops:
  5.0 4.0 %collective-permute-start.2 = (bf16[8,2,128,256]{3,2,1,0:T(8,128)(2,1)S(1)}, bf16[8,2,128,256]{3,2,1,0:T(8,128)(2,1)}, u32[]{:S(2)}, u32[]{:S(2)}) collective-permute-start(bf16[8,2,128,256]{3,2,1,0:T(8,128)(2,1)S(1)} %bitcast.19), channel_id=1, source_target_pairs={{0,56},{8,0},{16,8},{24,16},{32,24},{40,32},{48,40},{56,48},{64,12... | collective-permute-start | bytes 3145736 | tf_op jit(solution)/shard_map/ppermute | solution.py:272
  11.9 20.0 %collective-permute-done.l1_a.refs_1_ = bf16[8,2,128,256]{3,2,1,0:T(8,128)(2,1)} collective-permute-done((bf16[8,2,128,256]{3,2,1,0:T(8,128)(2,1)S(1)}, bf16[8,2,128,256]{3,2,1,0:T(8,128)(2,1)}, u32[]{:S(2)}, u32[]{:S(2)}) %collective-permute-start) | collective-permute-done | bytes 1048608 | tf_op jit(solution)/shard_map/ppermute | solution.py:272
  34.6 19.8 %collective-permute-done.7.l1_b.refs_1_ = bf16[8,2,128,256]{3,2,1,0:T(8,128)(2,1)} collective-permute-done((bf16[8,2,128,256]{3,2,1,0:T(8,128)(2,1)S(1)}, bf16[8,2,128,256]{3,2,1,0:T(8,128)(2,1)}, u32[]{:S(2)}, u32[]{:S(2)}) %collective-permute-start.7) | collective-permute-done | bytes 1048608 | tf_op jit(solution)/shard_map/ppermute | solution.py:272
  58.8 4.3 %shard_map.78 = (bf16[8,2,128,256]{3,2,1,0:T(8,128)(2,1)}, bf16[6,2,128,256]{3,2,1,0:T(8,128)(2,1)}, bf16[8,2,128,256]{3,2,1,0:T(8,128)(2,1)}) custom-call(s32[37]{0:T(128)} %concatenate.17.pick_ref, bf16[8,2,128,256]{3,2,1,0:T(8,128)(2,1)} %bitcast.20, bf16[8,2,128,256]{3,2,1,0:T(8,128)(2,1)} %collective-permute-done.l1_a.refs_1_, ...), custom_call_target="tpu_custom_call" | custom-call | bytes 6000000 | tf_op jit(solution)/shard_map/pallas_call | solution.py:280
  63.1 3.0 collective-permute-start.11
  66.1 10.8 %collective-permute-done.1.l2.l2_a.refs_2_ = bf16[8,2,128,256]{3,2,1,0:T(8,128)(2,1)S(1)} collective-permute-done((bf16[8,2,128,256]{3,2,1,0:T(8,128)(2,1)}, bf16[8,2,128,256]{3,2,1,0:T(8,128)(2,1)S(1)}, u32[]{:S(2)}, u32[]{:S(2)}) %collective-permute-start.1) | collective-permute-done | bytes 1048608 | tf_op jit(solution)/shard_map/ppermute | solution.py:272
  76.9 22.5 %collective-permute-done.16.l2_b.refs_2_ = bf16[8,2,128,256]{3,2,1,0:T(8,128)(2,1)} collective-permute-done((bf16[8,2,128,256]{3,2,1,0:T(8,128)(2,1)}, bf16[8,2,128,256]{3,2,1,0:T(8,128)(2,1)}, u32[]{:S(2)}, u32[]{:S(2)}) %collective-permute-start.16) | collective-permute-done | bytes 1048608 | tf_op jit(solution)/shard_map/ppermute | solution.py:272
  99.3 4.5 %shard_map.80 = (bf16[6,2,128,256]{3,2,1,0:T(8,128)(2,1)}, bf16[6,2,128,256]{3,2,1,0:T(8,128)(2,1)}, bf16[4,2,128,256]{3,2,1,0:T(8,128)(2,1)}, bf16[4,2,128,256]{3,2,1,0:T(8,128)(2,1)}, bf16[4,2,128,256]{3,2,1,0:T(8,128)(2,1)}) custom-call(s32[37]{0:T(128)} %concatenate.17.pick_ref, bf16[8,2,128,256]{3,2,1,0:T(8,128)(2,1)} %copy-done, ...), custom_call_target="tpu_custom_call" | custom-call | bytes 6000000 | tf_op jit(solution)/shard_map/pallas_call | solution.py:280
  112.3 3.4 %collective-permute-done.22.refs_2_ = bf16[2,2,32,512]{3,2,1,0:T(8,128)(2,1)S(1)} collective-permute-done((bf16[2,2,32,512]{3,2,1,0:T(8,128)(2,1)}, bf16[2,2,32,512]{3,2,1,0:T(8,128)(2,1)S(1)}, u32[]{:S(2)}, u32[]{:S(2)}) %collective-permute-start.22) | collective-permute-done | bytes 131104 | tf_op jit(solution)/shard_map/ppermute | solution.py:272
  122.0 4.2 %collective-permute-done.24.refs_1_ = bf16[2,2,32,512]{3,2,1,0:T(8,128)(2,1)S(1)} collective-permute-done((bf16[2,2,32,512]{3,2,1,0:T(8,128)(2,1)}, bf16[2,2,32,512]{3,2,1,0:T(8,128)(2,1)S(1)}, u32[]{:S(2)}, u32[]{:S(2)}) %collective-permute-start.24) | collective-permute-done | bytes 131104 | tf_op jit(solution)/shard_map/ppermute | solution.py:272
  134.5 3.9 %collective-permute-done.26.refs_2_.refs_3_.refs_4_ = bf16[2,2,32,512]{3,2,1,0:T(8,128)(2,1)S(1)} collective-permute-done((bf16[2,2,32,512]{3,2,1,0:T(8,128)(2,1)}, bf16[2,2,32,512]{3,2,1,0:T(8,128)(2,1)S(1)}, u32[]{:S(2)}, u32[]{:S(2)}) %collective-permute-start.26) | collective-permute-done | bytes 131104 | tf_op jit(solution)/shard_map/ppermute | solution.py:272
  144.4 3.1 collective-permute-start.29
  148.9 5.4 %collective-permute-start.33 = (bf16[6,2,128,256]{3,2,1,0:T(8,128)(2,1)}, bf16[6,2,128,256]{3,2,1,0:T(8,128)(2,1)S(1)}, u32[]{:S(2)}, u32[]{:S(2)}) collective-permute-start(bf16[6,2,128,256]{3,2,1,0:T(8,128)(2,1)} %get-tuple-element.45), channel_id=1, source_target_pairs={{0,56},{8,0},{16,8},{24,16},{32,24},{40,32},{48,40},{56,48},{64,12... | collective-permute-start | bytes 2359304 | tf_op jit(solution)/shard_map/ppermute | solution.py:272
  154.3 3.4 %shard_map.77 = (bf16[6,2,128,256]{3,2,1,0:T(8,128)(2,1)}, bf16[6,2,128,256]{3,2,1,0:T(8,128)(2,1)}) custom-call(s32[37]{0:T(128)} %concatenate.17.pick_ref, bf16[8,2,128,256]{3,2,1,0:T(8,128)(2,1)} %copy-done, bf16[8,2,128,256]{3,2,1,0:T(8,128)(2,1)} %copy-done.1), custom_call_target="tpu_custom_call" | custom-call | bytes 6000000 | tf_op jit(solution)/shard_map/pallas_call | solution.py:280
  160.8 9.4 %collective-permute-done.33.b3.refs_5_ = bf16[6,2,128,256]{3,2,1,0:T(8,128)(2,1)S(1)} collective-permute-done((bf16[6,2,128,256]{3,2,1,0:T(8,128)(2,1)}, bf16[6,2,128,256]{3,2,1,0:T(8,128)(2,1)S(1)}, u32[]{:S(2)}, u32[]{:S(2)}) %collective-permute-start.33) | collective-permute-done | bytes 786464 | tf_op jit(solution)/shard_map/ppermute | solution.py:272
  171.7 15.3 %collective-permute-done.6.b3.refs_5_ = bf16[6,2,128,256]{3,2,1,0:T(8,128)(2,1)S(1)} collective-permute-done((bf16[6,2,128,256]{3,2,1,0:T(8,128)(2,1)}, bf16[6,2,128,256]{3,2,1,0:T(8,128)(2,1)S(1)}, u32[]{:S(2)}, u32[]{:S(2)}) %collective-permute-start.6) | collective-permute-done | bytes 786464 | tf_op jit(solution)/shard_map/ppermute | solution.py:272
  187.0 3.5 %collective-permute-start.34 = (bf16[2,2,128,256]{3,2,1,0:T(8,128)(2,1)}, bf16[2,2,128,256]{3,2,1,0:T(8,128)(2,1)}, u32[]{:S(2)}, u32[]{:S(2)}) collective-permute-start(bf16[2,2,128,256]{3,2,1,0:T(8,128)(2,1)} %slice.54), channel_id=1, source_target_pairs={{0,56},{8,0},{16,8},{24,16},{32,24},{40,32},{48,40},{56,48},{64,12... | collective-permute-start | bytes 786440 | tf_op jit(solution)/shard_map/ppermute | solution.py:272
  208.6 3.3 %collective-permute-start.36 = (bf16[3,2,128,256]{3,2,1,0:T(8,128)(2,1)}, bf16[3,2,128,256]{3,2,1,0:T(8,128)(2,1)S(1)}, u32[]{:S(2)}, u32[]{:S(2)}) collective-permute-start(bf16[3,2,128,256]{3,2,1,0:T(8,128)(2,1)} %get-tuple-element.47), channel_id=1, source_target_pairs={{0,192},{8,200},{16,208},{24,216},{32,224},{40,232},{48,240},{56,2... | collective-permute-start | bytes 1179656 | tf_op jit(solution)/shard_map/ppermute | solution.py:272
  217.7 9.5 %collective-permute-start.14 = (bf16[3,2,128,256]{3,2,1,0:T(8,128)(2,1)}, bf16[3,2,128,256]{3,2,1,0:T(8,128)(2,1)S(1)}, u32[]{:S(2)}, u32[]{:S(2)}) collective-permute-start(bf16[3,2,128,256]{3,2,1,0:T(8,128)(2,1)} %get-tuple-element.34), channel_id=1, source_target_pairs={{0,192},{8,200},{16,208},{24,216},{32,224},{40,232},{48,240},{56,2... | collective-permute-start | bytes 1179656 | tf_op jit(solution)/shard_map/ppermute | solution.py:272
  228.3 4.9 %collective-permute-done.36.refs_12_ = bf16[3,2,128,256]{3,2,1,0:T(8,128)(2,1)S(1)} collective-permute-done((bf16[3,2,128,256]{3,2,1,0:T(8,128)(2,1)}, bf16[3,2,128,256]{3,2,1,0:T(8,128)(2,1)S(1)}, u32[]{:S(2)}, u32[]{:S(2)}) %collective-permute-start.36) | collective-permute-done | bytes 393248 | tf_op jit(solution)/shard_map/ppermute | solution.py:272
  234.1 16.5 %shard_map.87 = (f32[1024,256]{1,0:T(8,128)}, f32[8,128]{1,0:T(8,128)}) custom-call(s32[54]{0:T(128)} %get-tuple-element.71.code_ref, bf16[1024,512]{1,0:T(8,128)(2,1)} %q_ref.3, f32[1024,512]{1,0:T(8,128)} %refs_2_.1, bf16[8,2,128,256]{3,2,1,0:T(8,128)(2,1)} %bitcast.25, bf16[8,2,128,256]{3,2,1,0:T(8,128)(2,1)} %collective-permute-done.7.l1_b.refs_1_, ...), custom_call_target="tpu_custom_call" | custom-call | flops 2684354560 | bytes 4194304 | tf_op jit(solution)/shard_map/pallas_call | solution.py:431
  251.6 16.6 %shard_map.85 = (f32[1024,256]{1,0:T(8,128)}, f32[8,128]{1,0:T(8,128)}) custom-call(s32[54]{0:T(128)} %get-tuple-element.72.code_ref, bf16[1024,512]{1,0:T(8,128)(2,1)} %q_ref.3, f32[1024,512]{1,0:T(8,128)} %refs_2_.1, bf16[8,2,128,256]{3,2,1,0:T(8,128)(2,1)} %bitcast.21, bf16[8,2,128,256]{3,2,1,0:T(8,128)(2,1)} %collective-permute-done.l1_a.refs_1_, ...), custom_call_target="tpu_custom_call" | custom-call | flops 2684354560 | bytes 4194304 | tf_op jit(solution)/shard_map/pallas_call | solution.py:431
  269.0 37.2 %all_to_all.8 = f32[256,1,128]{2,1,0:T(1,128)} all-to-all(f32[256,1,128]{2,1,0:T(1,128)S(1)} %broadcast_in_dim.74), channel_id=1, replica_groups=mesh['ctx'=32,'head'=8] {'ctx','head'}, dimensions={0} | all-to-all | bytes 262144 | tf_op jit(solution)/shard_map/all_to_all | solution.py:460
  306.2 4.9 %finish.1 = (f32[1024,512]{1,0:T(8,128)}, f32[8,128]{1,0:T(8,128)}) custom-call(f32[256,128]{1,0:T(8,128)} %bitcast.28, f32[1024,256]{1,0:T(8,128)} %get-tuple-element.50.refs_0_, f32[1024,256]{1,0:T(8,128)} %get-tuple-element.51.refs_1_, f32[1024,512]{1,0:T(8,128)} %refs_2_.1), custom_call_target="tpu_custom_call" | custom-call | tf_op jit(solution)/shard_map/finish/pallas_call | solution.py:465
  (167 shorter events, 77.7 us)
Async XLA Ops:
  2.5 29.4 %collective-permute-start = (bf16[8,2,128,256]{3,2,1,0:T(8,128)(2,1)S(1)}, bf16[8,2,128,256]{3,2,1,0:T(8,128)(2,1)}, u32[]{:S(2)}, u32[]{:S(2)}) collective-permute-start(bf16[8,2,128,256]{3,2,1,0:T(8,128)(2,1)S(1)} %bitcast.18), channel_id=1, source_target_pairs={{0,8},{8,16},{16,24},{24,32},{32,40},{40,48},{48,56},{56,0},{64,72... | collective-permute-start | bytes 3145736 | tf_op jit(solution)/shard_map/ppermute | solution.py:272
  5.0 26.9 %collective-permute-start.2 = (bf16[8,2,128,256]{3,2,1,0:T(8,128)(2,1)S(1)}, bf16[8,2,128,256]{3,2,1,0:T(8,128)(2,1)}, u32[]{:S(2)}, u32[]{:S(2)}) collective-permute-start(bf16[8,2,128,256]{3,2,1,0:T(8,128)(2,1)S(1)} %bitcast.19), channel_id=1, source_target_pairs={{0,56},{8,0},{16,8},{24,16},{32,24},{40,32},{48,40},{56,48},{64,12... | collective-permute-start | bytes 3145736 | tf_op jit(solution)/shard_map/ppermute | solution.py:272
  9.1 45.3 %collective-permute-start.7 = (bf16[8,2,128,256]{3,2,1,0:T(8,128)(2,1)S(1)}, bf16[8,2,128,256]{3,2,1,0:T(8,128)(2,1)}, u32[]{:S(2)}, u32[]{:S(2)}) collective-permute-start(bf16[8,2,128,256]{3,2,1,0:T(8,128)(2,1)S(1)} %bitcast.22), channel_id=1, source_target_pairs={{0,8},{8,16},{16,24},{24,32},{32,40},{40,48},{48,56},{56,0},{64,72... | collective-permute-start | bytes 3145736 | tf_op jit(solution)/shard_map/ppermute | solution.py:272
  9.2 45.2 %collective-permute-start.8 = (bf16[8,2,128,256]{3,2,1,0:T(8,128)(2,1)S(1)}, bf16[8,2,128,256]{3,2,1,0:T(8,128)(2,1)}, u32[]{:S(2)}, u32[]{:S(2)}) collective-permute-start(bf16[8,2,128,256]{3,2,1,0:T(8,128)(2,1)S(1)} %bitcast.23), channel_id=1, source_target_pairs={{0,56},{8,0},{16,8},{24,16},{32,24},{40,32},{48,40},{56,48},{64,12... | collective-permute-start | bytes 3145736 | tf_op jit(solution)/shard_map/ppermute | solution.py:272
  31.9 44.9 %collective-permute-start.1 = (bf16[8,2,128,256]{3,2,1,0:T(8,128)(2,1)}, bf16[8,2,128,256]{3,2,1,0:T(8,128)(2,1)S(1)}, u32[]{:S(2)}, u32[]{:S(2)}) collective-permute-start(bf16[8,2,128,256]{3,2,1,0:T(8,128)(2,1)} %collective-permute-done.l1_a.refs_1_), channel_id=1, source_target_pairs={{0,8},{8,16},{16,24},{24,32},{32,40},{40,48},{48,56},{56,0},{64,72... | collective-permute-start | bytes 3145736 | tf_op jit(solution)/shard_map/ppermute | solution.py:272
  31.9 44.9 %collective-permute-start.3 = (bf16[8,2,128,256]{3,2,1,0:T(8,128)(2,1)}, bf16[8,2,128,256]{3,2,1,0:T(8,128)(2,1)S(1)}, u32[]{:S(2)}, u32[]{:S(2)}) collective-permute-start(bf16[8,2,128,256]{3,2,1,0:T(8,128)(2,1)} %collective-permute-done.2.r1_a.refs_7_), channel_id=1, source_target_pairs={{0,56},{8,0},{16,8},{24,16},{32,24},{40,32},{48,40},{56,48},{64,12... | collective-permute-start | bytes 3145736 | tf_op jit(solution)/shard_map/ppermute | solution.py:272
  54.4 44.9 %collective-permute-start.16 = (bf16[8,2,128,256]{3,2,1,0:T(8,128)(2,1)}, bf16[8,2,128,256]{3,2,1,0:T(8,128)(2,1)}, u32[]{:S(2)}, u32[]{:S(2)}) collective-permute-start(bf16[8,2,128,256]{3,2,1,0:T(8,128)(2,1)} %collective-permute-done.7.l1_b.refs_1_), channel_id=1, source_target_pairs={{0,8},{8,16},{16,24},{24,32},{32,40},{40,48},{48,56},{56,0},{64,72... | collective-permute-start | bytes 3145736 | tf_op jit(solution)/shard_map/ppermute | solution.py:272
  54.4 44.9 %collective-permute-start.17 = (bf16[8,2,128,256]{3,2,1,0:T(8,128)(2,1)}, bf16[8,2,128,256]{3,2,1,0:T(8,128)(2,1)}, u32[]{:S(2)}, u32[]{:S(2)}) collective-permute-start(bf16[8,2,128,256]{3,2,1,0:T(8,128)(2,1)} %collective-permute-done.8.r1_b.refs_7_), channel_id=1, source_target_pairs={{0,56},{8,0},{16,8},{24,16},{32,24},{40,32},{48,40},{56,48},{64,12... | collective-permute-start | bytes 3145736 | tf_op jit(solution)/shard_map/ppermute | solution.py:272
  63.1 96.2 %collective-permute-start.11 = (bf16[6,2,128,256]{3,2,1,0:T(8,128)(2,1)}, bf16[6,2,128,256]{3,2,1,0:T(8,128)(2,1)}, u32[]{:S(2)}, u32[]{:S(2)}) collective-permute-start(bf16[6,2,128,256]{3,2,1,0:T(8,128)(2,1)} %get-tuple-element.32), channel_id=1, source_target_pairs={{0,128},{8,136},{16,144},{24,152},{32,160},{40,168},{48,176},{56,1... | collective-permute-start | bytes 2359304 | tf_op jit(solution)/shard_map/ppermute | solution.py:272
  103.8 55.5 %collective-permute-start.31 = (bf16[6,2,128,256]{3,2,1,0:T(8,128)(2,1)}, bf16[6,2,128,256]{3,2,1,0:T(8,128)(2,1)S(1)}, u32[]{:S(2)}, u32[]{:S(2)}) collective-permute-start(bf16[6,2,128,256]{3,2,1,0:T(8,128)(2,1)} %get-tuple-element.44), channel_id=1, source_target_pairs={{0,8},{8,16},{16,24},{24,32},{32,40},{40,48},{48,56},{56,0},{64,72... | collective-permute-start | bytes 2359304 | tf_op jit(solution)/shard_map/ppermute | solution.py:272
  148.9 21.3 %collective-permute-start.33 = (bf16[6,2,128,256]{3,2,1,0:T(8,128)(2,1)}, bf16[6,2,128,256]{3,2,1,0:T(8,128)(2,1)S(1)}, u32[]{:S(2)}, u32[]{:S(2)}) collective-permute-start(bf16[6,2,128,256]{3,2,1,0:T(8,128)(2,1)} %get-tuple-element.45), channel_id=1, source_target_pairs={{0,56},{8,0},{16,8},{24,16},{32,24},{40,32},{48,40},{56,48},{64,12... | collective-permute-start | bytes 2359304 | tf_op jit(solution)/shard_map/ppermute | solution.py:272
  157.7 44.5 %collective-permute-start.10 = (bf16[8,2,128,256]{3,2,1,0:T(8,128)(2,1)}, bf16[8,2,128,256]{3,2,1,0:T(8,128)(2,1)}, u32[]{:S(2)}, u32[]{:S(2)}) collective-permute-start(bf16[8,2,128,256]{3,2,1,0:T(8,128)(2,1)} %get-tuple-element.31), channel_id=1, source_target_pairs={{0,192},{8,200},{16,208},{24,216},{32,224},{40,232},{48,240},{56,2... | collective-permute-start | bytes 3145736 | tf_op jit(solution)/shard_map/ppermute | solution.py:272
  157.8 44.4 %collective-permute-start.9 = (bf16[8,2,128,256]{3,2,1,0:T(8,128)(2,1)}, bf16[8,2,128,256]{3,2,1,0:T(8,128)(2,1)}, u32[]{:S(2)}, u32[]{:S(2)}) collective-permute-start(bf16[8,2,128,256]{3,2,1,0:T(8,128)(2,1)} %get-tuple-element.30), channel_id=1, source_target_pairs={{0,64},{8,72},{16,80},{24,88},{32,96},{40,104},{48,112},{56,120},{... | collective-permute-start | bytes 3145736 | tf_op jit(solution)/shard_map/ppermute | solution.py:272
  159.3 27.7 %collective-permute-start.6 = (bf16[6,2,128,256]{3,2,1,0:T(8,128)(2,1)}, bf16[6,2,128,256]{3,2,1,0:T(8,128)(2,1)S(1)}, u32[]{:S(2)}, u32[]{:S(2)}) collective-permute-start(bf16[6,2,128,256]{3,2,1,0:T(8,128)(2,1)} %get-tuple-element.29), channel_id=1, source_target_pairs={{0,56},{8,0},{16,8},{24,16},{32,24},{40,32},{48,40},{56,48},{64,12... | collective-permute-start | bytes 2359304 | tf_op jit(solution)/shard_map/ppermute | solution.py:272
  159.3 27.7 %collective-permute-start.4 = (bf16[6,2,128,256]{3,2,1,0:T(8,128)(2,1)}, bf16[6,2,128,256]{3,2,1,0:T(8,128)(2,1)S(1)}, u32[]{:S(2)}, u32[]{:S(2)}) collective-permute-start(bf16[6,2,128,256]{3,2,1,0:T(8,128)(2,1)} %get-tuple-element.28), channel_id=1, source_target_pairs={{0,8},{8,16},{16,24},{24,32},{32,40},{40,48},{48,56},{56,0},{64,72... | collective-permute-start | bytes 2359304 | tf_op jit(solution)/shard_map/ppermute | solution.py:272
  170.2 37.0 %collective-permute-start.18 = (bf16[4,2,128,256]{3,2,1,0:T(8,128)(2,1)}, bf16[4,2,128,256]{3,2,1,0:T(8,128)(2,1)}, u32[]{:S(2)}, u32[]{:S(2)}) collective-permute-start(bf16[4,2,128,256]{3,2,1,0:T(8,128)(2,1)} %get-tuple-element.36), channel_id=1, source_target_pairs={{0,64},{8,72},{16,80},{24,88},{32,96},{40,104},{48,112},{56,120},{... | collective-permute-start | bytes 1572872 | tf_op jit(solution)/shard_map/ppermute | solution.py:272
  187.0 16.8 %collective-permute-start.34 = (bf16[2,2,128,256]{3,2,1,0:T(8,128)(2,1)}, bf16[2,2,128,256]{3,2,1,0:T(8,128)(2,1)}, u32[]{:S(2)}, u32[]{:S(2)}) collective-permute-start(bf16[2,2,128,256]{3,2,1,0:T(8,128)(2,1)} %slice.54), channel_id=1, source_target_pairs={{0,56},{8,0},{16,8},{24,16},{32,24},{40,32},{48,40},{56,48},{64,12... | collective-permute-start | bytes 786440 | tf_op jit(solution)/shard_map/ppermute | solution.py:272
  202.3 15.5 %collective-permute-start.20 = (bf16[4,2,128,256]{3,2,1,0:T(8,128)(2,1)}, bf16[4,2,128,256]{3,2,1,0:T(8,128)(2,1)}, u32[]{:S(2)}, u32[]{:S(2)}) collective-permute-start(bf16[4,2,128,256]{3,2,1,0:T(8,128)(2,1)} %get-tuple-element.38), channel_id=1, source_target_pairs={{0,128},{8,136},{16,144},{24,152},{32,160},{40,168},{48,176},{56,1... | collective-permute-start | bytes 1572872 | tf_op jit(solution)/shard_map/ppermute | solution.py:272
  207.2 20.2 %collective-permute-start.35 = (bf16[3,2,128,256]{3,2,1,0:T(8,128)(2,1)}, bf16[3,2,128,256]{3,2,1,0:T(8,128)(2,1)S(1)}, u32[]{:S(2)}, u32[]{:S(2)}) collective-permute-start(bf16[3,2,128,256]{3,2,1,0:T(8,128)(2,1)} %get-tuple-element.46), channel_id=1, source_target_pairs={{0,64},{8,72},{16,80},{24,88},{32,96},{40,104},{48,112},{56,120},{... | collective-permute-start | bytes 1179656 | tf_op jit(solution)/shard_map/ppermute | solution.py:272
  208.6 24.6 %collective-permute-start.36 = (bf16[3,2,128,256]{3,2,1,0:T(8,128)(2,1)}, bf16[3,2,128,256]{3,2,1,0:T(8,128)(2,1)S(1)}, u32[]{:S(2)}, u32[]{:S(2)}) collective-permute-start(bf16[3,2,128,256]{3,2,1,0:T(8,128)(2,1)} %get-tuple-element.47), channel_id=1, source_target_pairs={{0,192},{8,200},{16,208},{24,216},{32,224},{40,232},{48,240},{56,2... | collective-permute-start | bytes 1179656 | tf_op jit(solution)/shard_map/ppermute | solution.py:272
  212.0 21.2 %collective-permute-start.37 = (bf16[3,2,128,256]{3,2,1,0:T(8,128)(2,1)}, bf16[3,2,128,256]{3,2,1,0:T(8,128)(2,1)S(1)}, u32[]{:S(2)}, u32[]{:S(2)}) collective-permute-start(bf16[3,2,128,256]{3,2,1,0:T(8,128)(2,1)} %get-tuple-element.48), channel_id=1, source_target_pairs={{0,128},{8,136},{16,144},{24,152},{32,160},{40,168},{48,176},{56,1... | collective-permute-start | bytes 1179656 | tf_op jit(solution)/shard_map/ppermute | solution.py:272
  216.1 34.4 %collective-permute-start.13 = (bf16[3,2,128,256]{3,2,1,0:T(8,128)(2,1)}, bf16[3,2,128,256]{3,2,1,0:T(8,128)(2,1)S(1)}, u32[]{:S(2)}, u32[]{:S(2)}) collective-permute-start(bf16[3,2,128,256]{3,2,1,0:T(8,128)(2,1)} %get-tuple-element.33), channel_id=1, source_target_pairs={{0,64},{8,72},{16,80},{24,88},{32,96},{40,104},{48,112},{56,120},{... | collective-permute-start | bytes 1179656 | tf_op jit(solution)/shard_map/ppermute | solution.py:272
  217.7 32.9 %collective-permute-start.14 = (bf16[3,2,128,256]{3,2,1,0:T(8,128)(2,1)}, bf16[3,2,128,256]{3,2,1,0:T(8,128)(2,1)S(1)}, u32[]{:S(2)}, u32[]{:S(2)}) collective-permute-start(bf16[3,2,128,256]{3,2,1,0:T(8,128)(2,1)} %get-tuple-element.34), channel_id=1, source_target_pairs={{0,192},{8,200},{16,208},{24,216},{32,224},{40,232},{48,240},{56,2... | collective-permute-start | bytes 1179656 | tf_op jit(solution)/shard_map/ppermute | solution.py:272
  227.4 23.2 %collective-permute-start.15 = (bf16[3,2,128,256]{3,2,1,0:T(8,128)(2,1)}, bf16[3,2,128,256]{3,2,1,0:T(8,128)(2,1)S(1)}, u32[]{:S(2)}, u32[]{:S(2)}) collective-permute-start(bf16[3,2,128,256]{3,2,1,0:T(8,128)(2,1)} %get-tuple-element.35), channel_id=1, source_target_pairs={{0,128},{8,136},{16,144},{24,152},{32,160},{40,168},{48,176},{56,1... | collective-permute-start | bytes 1179656 | tf_op jit(solution)/shard_map/ppermute | solution.py:272
  (45 other events, 772.0 us)

commit v2 on v1

--- a/solution.py
+++ b/solution.py
@@ -59,7 +59,7 @@
 NY, NZ = 4, 8
 CHUNKS = ((0, 2), (2, 2))
 CALLS = len(CHUNKS)
-OWN, L1, _, _, _, _, _, R1, YP, YM, _, LYP, _, _, MP, _, _ = range(17)
+OWN, L1, _, _, _, _, _, R1, YP, YM, _, LYP, _, _, MP, MM, M2, FP, _, _ = range(20)
 
 
 def start_choice(arrays, ids, code, dst, sem):
@@ -73,8 +73,8 @@
 
 def attention_kernel(nblocks, chunk, narrays, code_ref, q_ref, vec_ref, *refs):
     arrays = refs[:narrays]
-    pieces = refs[narrays : narrays + NY]
-    out_ref, stat_ref, kvbuf, sems, acc = refs[narrays + NY :]
+    quarter = refs[narrays]
+    out_ref, stat_ref, kvbuf, sems, acc = refs[narrays + 1 :]
     b = pl.program_id(0)
     width = q_ref.shape[1]
     table = nblocks * 6
@@ -86,12 +86,17 @@
     def globals_in(slot):
         copies = []
         cols = pl.ds(chunk[0] * HD, width)
-        for i in range(NY):
+        part = BS // NY
+        for i, array in enumerate((None, MP, M2, MM)):
             rows = pl.multiple_of(code_ref[table + 2 + i], BS // NY)
             for g in range(2):
                 dst = kvbuf.at[slot, :, pl.ds((3 + g) * BS + rows, BS // NY)]
                 sem = sems.at[slot, LIST + 2 * i + g]
-                copies.append(pltpu.make_async_copy(pieces[i].at[g, :, :, cols], dst, sem))
+                if array is None:
+                    src = quarter.at[g, :, :, cols]
+                else:
+                    src = arrays[array].at[4, :, pl.ds((2 * g + chunk[1]) * part, part)]
+                copies.append(pltpu.make_async_copy(src, dst, sem))
         return copies
 
     def start(blk, slot):
@@ -184,11 +189,27 @@
     run_copies(third_hop(pick_ref, l2, r2, plus, minus), sems)
 
 
-def second_kernel(pick_ref, l2_a, r2_a, l2_b, r2_b, plus, minus, yp, y2, ym, sems):
+def second_kernel(pick_ref, l2_a, r2_a, l2_b, r2_b, quarter, plus, minus, yp, y2, ym, sems):
     plan = third_hop(pick_ref, l2_b, r2_b, plus, minus)
     for row, out in enumerate((yp, y2, ym)):
         for i, src in enumerate((l2_a, r2_a, l2_b, r2_b)):
             plan.append((src.at[pick_ref[12 + row * 5 + 3 + i % 2]], out.at[i]))
+        part, half = quarter.shape[2], quarter.shape[3] // 2
+        for g in range(2):
+            for k in range(2):
+                plan.append(
+                    (
+                        quarter.at[g, :, :, pl.ds(k * half, half)],
+                        out.at[4, :, pl.ds((2 * g + k) * part, part)],
+                    )
+                )
+    run_copies(plan, sems)
+
+
+def half_kernel(a3, b3, yp, y2, ym, sems):
+    plan = []
+    for row, out in enumerate((yp, y2, ym)):
+        plan += [(a3.at[row + 1], out.at[0]), (b3.at[row + 1], out.at[1])]
     run_copies(plan, sems)
 
 
@@ -250,8 +271,8 @@
         beta = jnp.sqrt(square * (1.0 / count) + 1e-06)
         ab[0:1, :] = jnp.broadcast_to(alpha, (1, 128))
         ab[1:2, :] = jnp.broadcast_to(1.0 / beta, (1, 128))
-        lane = lax.broadcasted_iota(jnp.int32, coef_ref.shape, 1)
-        coef_ref[...] = jnp.where(lane == 0, alpha, beta)
+        coef_ref[0] = alpha[0, 0]
+        coef_ref[1] = beta[0, 0]
 
     alpha = ab[0:1, 0:1]
     inv = ab[1:2, 0:1]
@@ -339,6 +360,9 @@
         edge_slot = chunk * 4 + 3
         far = jnp.where(late, LYP, jnp.where(second, MP, YP)) + row
         base = jnp.where(late, 0, jnp.where(second, chunk * 2 - 3, chunk * jnp.where(row == 2, 3, 4)))
+        if chunk == 0:
+            far = jnp.where(dz == 4, FP + row, far)
+            base = jnp.where(dz == 4, -2, base)
         rand_code = jnp.where(dy == 0, dz * 8 + near_slot, far * 8 + order + base).reshape(nblocks, 3)
         left = jnp.where(
             block == 0, jnp.where(my_z == 0, YP * 8 + edge_slot, L1 * 8 + nblocks - 1), block - 1
@@ -380,9 +404,6 @@
         functools.partial(choose_kernel, 35), picks,
         (close, close, hop_left, hop_left, hop_left, hop_right, hop_right, close), (piece,), 2,
     )
-    pieces = (
-        quarter, send(quarter, y_shift(1)), send(quarter, y_shift(2)), send(quarter, y_shift(-1))
-    )
     cw = CHUNKS[0][1] * HD
 
     def slots(count):
@@ -407,21 +428,23 @@
     plus, minus = pack(third_kernel, picks, (l2[0], r2[0]), (slots(6), slots(6)), 12)
     a3, b3 = send(plus, z_shift(1)), send(minus, z_shift(-1))
     plus, minus, *two = pack(
-        second_kernel, picks, (l2[0], r2[0], l2[1], r2[1]),
-        (slots(6), slots(6)) + (slots(4),) * 3, 24,
+        second_kernel, picks, (l2[0], r2[0], l2[1], r2[1], quarter),
+        (slots(6), slots(6)) + (slots(5),) * 3, 36,
     )
     y2 = rows_of(two)
     c3, d3 = send(plus, z_shift(1)), send(minus, z_shift(-1))
     a4, b4 = send(a3[4:6], z_shift(1)), send(b3[4:6], z_shift(-1))
     c4, d4 = send(c3[4:6], z_shift(1)), send(d3[4:6], z_shift(-1))
-    y3a = rows_of(pack(late_kernel, None, (a3, b3, a4, b4), (slots(3),) * 3, 9))
+    y3a = rows_of(pack(half_kernel, None, (a3, b3), (slots(2),) * 3, 6))
+    y4a = rows_of((a4[1:2], b4[0:1], b4[1:2]))
     y3b = rows_of(pack(late_kernel, None, (c3, d3, c4, d4), (slots(3),) * 3, 9))
 
     def by_code(y):
         return (y[0], y[2], y[1])
 
     sources = (
-        (own[0], l1[0], l2[0], a3, a4, b3, r2[0], r1[0]) + by_code(y1) + by_code(y3a) + by_code(y2),
+        (own[0], l1[0], l2[0], a3, a4, b3, r2[0], r1[0]) + by_code(y1) + by_code(y3a) + by_code(y2)
+        + by_code(y4a),
         (own[1], l1[1], l2[1], c3, c4, d3, r2[1], r1[1]) + by_code(y1) + by_code(y3b) + by_code(y2),
     )
     products = []
@@ -438,7 +461,7 @@
                 num_scalar_prefetch=1,
                 grid=(nblocks,),
                 in_specs=[pl.BlockSpec((BS, cw), lambda b, *_, k=k: (b, k))] * 2
-                + [ANY] * (len(arrays) + NY),
+                + [ANY] * (len(arrays) + 1),
                 out_specs=(
                     pl.BlockSpec((BS, cw), lambda b, *_: (b, 0)),
                     pl.BlockSpec((8, 128), lambda b, *_: (0, 0)),
@@ -453,7 +476,7 @@
                 flops=10 * rows * keys * cw, bytes_accessed=16 * rows * cw,
                 transcendentals=rows * keys * (cw // HD),
             ),
-        )(codes[k], queries, lanczos_vec, *arrays, *pieces)
+        )(codes[k], queries, lanczos_vec, *arrays, quarter)
         products.append(product)
         stats.append(stat)
     sent = jnp.broadcast_to(sum(stats)[:1], (nctx * nhead, 128))
@@ -466,15 +489,15 @@
         functools.partial(finish_kernel, count),
         out_shape=(
             jax.ShapeDtypeStruct((rows, width), jnp.float32),
-            jax.ShapeDtypeStruct((8, 128), jnp.float32),
+            jax.ShapeDtypeStruct((2,), jnp.float32),
         ),
         grid=(4,),
         in_specs=[pl.BlockSpec((nctx * nhead, 128), lambda i: (0, 0))] + part_specs + [fin_spec],
-        out_specs=(fin_spec, pl.BlockSpec((8, 128), lambda i: (0, 0))),
+        out_specs=(fin_spec, pl.BlockSpec(memory_space=pltpu.SMEM)),
         scratch_shapes=[pltpu.VMEM((8, 128), jnp.float32)],
         name="finish",
     )(gathered, *products, lanczos_vec)
-    return next_vec, coef[0, :2]
+    return next_vec, coef
 
 
 def solution(mesh):

time: 313 us -> 301 us (0.962)
  waiting for transfers between devices: 116 us -> 128 us
  starting transfers between devices: 68 us -> 58 us
  local copies, waits for them, and re-layouts: 20.7 us -> 13.3 us
  blocking collectives: 37.2 us -> 33.6 us
    ppermute x38, waiting for transfers between devices: 116 us -> 128 us  [send(): return lax.ppermute(x, 'ctx', pairs)]
    ppermute x38, starting transfers between devices: 68 us -> 58 us  [send(): return lax.ppermute(x, 'ctx', pairs)]
    all_to_all x1, blocking collectives: 37.2 us -> 33.6 us  [whole_step(): gathered = lax.all_to_all(sent, ('ctx', 'head'), 0, 0, tiled=True)]
  transfers between devices with their start and end apart: 38 -> 38, of which waited for: 14 -> 16; matrix products, arithmetic and copies ran while one was open for 5% -> 3% of each run, Pallas kernels for 14% -> 14%
where the time goes in v2:
time: 301 us
  waiting for transfers between devices  128 us (43%)
  Pallas kernels  64.8 us (22%)
  starting transfers between devices  58 us (19%)
  blocking collectives  33.6 us (11%)
  local copies, waits for them, and re-layouts  13.3 us (4%)
    ppermute x38, waiting for transfers between devices, send(): return lax.ppermute(x, 'ctx', pairs)  128 us
    ppermute x38, starting transfers between devices, send(): return lax.ppermute(x, 'ctx', pairs)  58 us
    all_to_all x1, blocking collectives, whole_step(): gathered = lax.all_to_all(sent, ('ctx', 'head'), 0, 0, tiled=True)  33.6 us
    pallas_call x2, Pallas kernels, whole_step(): pl.pallas_call(functools.partial(attention_kernel, nblocks, (CHUNKS[k][0]...  33.5 us
    pallas_call x9, Pallas kernels, pack(): pl.pallas_call(kernel, out_shape=tuple((jax.ShapeDtypeStruct(shape, jnp.b...  26.4 us
  transfers between devices with their start and end apart: 38, of which 16 were waited for; matrix products, arithmetic and copies ran while one was open for 3% of the time, Pallas kernels for 14%

profile of v2, /device:TPU:1, one launch (start us, length us, event | category | flops | bytes accessed | tf_op | source)
XLA Modules:
  0.0 300.7 jit_solution(4017460101157170802)
XLA Ops:
  5.0 4.0 %collective-permute-start.2 = (bf16[8,2,128,256]{3,2,1,0:T(8,128)(2,1)S(1)}, bf16[8,2,128,256]{3,2,1,0:T(8,128)(2,1)}, u32[]{:S(2)}, u32[]{:S(2)}) collective-permute-start(bf16[8,2,128,256]{3,2,1,0:T(8,128)(2,1)S(1)} %bitcast.21), channel_id=1, source_target_pairs={{0,56},{8,0},{16,8},{24,16},{32,24},{40,32},{48,40},{56,48},{64,12... | collective-permute-start | bytes 3145736 | tf_op jit(solution)/shard_map/ppermute | solution.py:293
  17.6 4.4 %collective-permute-done.17.refs_1_ = bf16[2,2,32,512]{3,2,1,0:T(8,128)(2,1)S(1)} collective-permute-done((bf16[2,2,32,512]{3,2,1,0:T(8,128)(2,1)}, bf16[2,2,32,512]{3,2,1,0:T(8,128)(2,1)S(1)}, u32[]{:S(2)}, u32[]{:S(2)}) %collective-permute-start.17) | collective-permute-done | bytes 131104 | tf_op jit(solution)/shard_map/ppermute | solution.py:293
  23.6 3.9 %collective-permute-done.18.refs_2_ = bf16[2,2,32,512]{3,2,1,0:T(8,128)(2,1)S(1)} collective-permute-done((bf16[2,2,32,512]{3,2,1,0:T(8,128)(2,1)}, bf16[2,2,32,512]{3,2,1,0:T(8,128)(2,1)S(1)}, u32[]{:S(2)}, u32[]{:S(2)}) %collective-permute-start.18) | collective-permute-done | bytes 131104 | tf_op jit(solution)/shard_map/ppermute | solution.py:293
  29.0 2.9 collective-permute-done.l1_a.refs_1_
  34.6 19.8 %collective-permute-done.7.l1_b.refs_1_ = bf16[8,2,128,256]{3,2,1,0:T(8,128)(2,1)} collective-permute-done((bf16[8,2,128,256]{3,2,1,0:T(8,128)(2,1)S(1)}, bf16[8,2,128,256]{3,2,1,0:T(8,128)(2,1)}, u32[]{:S(2)}, u32[]{:S(2)}) %collective-permute-start.7) | collective-permute-done | bytes 1048608 | tf_op jit(solution)/shard_map/ppermute | solution.py:293
  60.0 42.0 %collective-permute-done.20.refs_1_ = bf16[2,2,32,512]{3,2,1,0:T(8,128)(2,1)S(1)} collective-permute-done((bf16[2,2,32,512]{3,2,1,0:T(8,128)(2,1)}, bf16[2,2,32,512]{3,2,1,0:T(8,128)(2,1)S(1)}, u32[]{:S(2)}, u32[]{:S(2)}) %collective-permute-start.20) | collective-permute-done | bytes 131104 | tf_op jit(solution)/shard_map/ppermute | solution.py:293
  111.6 5.9 %collective-permute-done.22.refs_2_.refs_3_.refs_4_ = bf16[2,2,32,512]{3,2,1,0:T(8,128)(2,1)S(1)} collective-permute-done((bf16[2,2,32,512]{3,2,1,0:T(8,128)(2,1)}, bf16[2,2,32,512]{3,2,1,0:T(8,128)(2,1)S(1)}, u32[]{:S(2)}, u32[]{:S(2)}) %collective-permute-start.22) | collective-permute-done | bytes 131104 | tf_op jit(solution)/shard_map/ppermute | solution.py:293
  118.5 4.3 %shard_map.78 = (bf16[8,2,128,256]{3,2,1,0:T(8,128)(2,1)}, bf16[6,2,128,256]{3,2,1,0:T(8,128)(2,1)}, bf16[8,2,128,256]{3,2,1,0:T(8,128)(2,1)}) custom-call(s32[37]{0:T(128)} %concatenate.17.pick_ref, bf16[8,2,128,256]{3,2,1,0:T(8,128)(2,1)} %bitcast.22, bf16[8,2,128,256]{3,2,1,0:T(8,128)(2,1)} %collective-permute-done.l1_a.refs_1_, ...), custom_call_target="tpu_custom_call" | custom-call | bytes 6000000 | tf_op jit(solution)/shard_map/pallas_call | solution.py:301
  124.2 2.9 collective-permute-start.11
  130.6 4.8 %shard_map.84 = (bf16[6,2,128,256]{3,2,1,0:T(8,128)(2,1)}, bf16[6,2,128,256]{3,2,1,0:T(8,128)(2,1)}, bf16[5,2,128,256]{3,2,1,0:T(8,128)(2,1)}, bf16[5,2,128,256]{3,2,1,0:T(8,128)(2,1)}, bf16[5,2,128,256]{3,2,1,0:T(8,128)(2,1)}) custom-call(s32[37]{0:T(128)} %concatenate.17.pick_ref, bf16[8,2,128,256]{3,2,1,0:T(8,128)(2,1)} %copy-done, ...), custom_call_target="tpu_custom_call" | custom-call | bytes 6000000 | tf_op jit(solution)/shard_map/pallas_call | solution.py:301
  135.5 4.7 %collective-permute-start.31 = (bf16[6,2,128,256]{3,2,1,0:T(8,128)(2,1)}, bf16[6,2,128,256]{3,2,1,0:T(8,128)(2,1)S(1)}, u32[]{:S(2)}, u32[]{:S(2)}) collective-permute-start(bf16[6,2,128,256]{3,2,1,0:T(8,128)(2,1)} %get-tuple-element.42), channel_id=1, source_target_pairs={{0,8},{8,16},{16,24},{24,32},{32,40},{40,48},{48,56},{56,0},{64,72... | collective-permute-start | bytes 2359304 | tf_op jit(solution)/shard_map/ppermute | solution.py:293
  140.2 3.4 %shard_map.77 = (bf16[6,2,128,256]{3,2,1,0:T(8,128)(2,1)}, bf16[6,2,128,256]{3,2,1,0:T(8,128)(2,1)}) custom-call(s32[37]{0:T(128)} %concatenate.17.pick_ref, bf16[8,2,128,256]{3,2,1,0:T(8,128)(2,1)} %copy-done, bf16[8,2,128,256]{3,2,1,0:T(8,128)(2,1)} %copy-done.1), custom_call_target="tpu_custom_call" | custom-call | bytes 6000000 | tf_op jit(solution)/shard_map/pallas_call | solution.py:301
  146.9 4.9 %collective-permute-done.31.a3.refs_3_ = bf16[6,2,128,256]{3,2,1,0:T(8,128)(2,1)S(1)} collective-permute-done((bf16[6,2,128,256]{3,2,1,0:T(8,128)(2,1)}, bf16[6,2,128,256]{3,2,1,0:T(8,128)(2,1)S(1)}, u32[]{:S(2)}, u32[]{:S(2)}) %collective-permute-start.31) | collective-permute-done | bytes 786464 | tf_op jit(solution)/shard_map/ppermute | solution.py:293
  154.9 3.1 %collective-permute-start.4 = (bf16[6,2,128,256]{3,2,1,0:T(8,128)(2,1)}, bf16[6,2,128,256]{3,2,1,0:T(8,128)(2,1)S(1)}, u32[]{:S(2)}, u32[]{:S(2)}) collective-permute-start(bf16[6,2,128,256]{3,2,1,0:T(8,128)(2,1)} %get-tuple-element.26), channel_id=1, source_target_pairs={{0,8},{8,16},{16,24},{24,32},{32,40},{40,48},{48,56},{56,0},{64,72... | collective-permute-start | bytes 2359304 | tf_op jit(solution)/shard_map/ppermute | solution.py:293
  158.0 13.7 %collective-permute-done.6.b3.refs_5_ = bf16[6,2,128,256]{3,2,1,0:T(8,128)(2,1)S(1)} collective-permute-done((bf16[6,2,128,256]{3,2,1,0:T(8,128)(2,1)}, bf16[6,2,128,256]{3,2,1,0:T(8,128)(2,1)S(1)}, u32[]{:S(2)}, u32[]{:S(2)}) %collective-permute-start.6) | collective-permute-done | bytes 786464 | tf_op jit(solution)/shard_map/ppermute | solution.py:293
  175.4 3.1 %collective-permute-start.32 = (bf16[2,2,128,256]{3,2,1,0:T(8,128)(2,1)}, bf16[2,2,128,256]{3,2,1,0:T(8,128)(2,1)S(1)}, u32[]{:S(2)}, u32[]{:S(2)}) collective-permute-start(bf16[2,2,128,256]{3,2,1,0:T(8,128)(2,1)} %slice.64), channel_id=1, source_target_pairs={{0,8},{8,16},{16,24},{24,32},{32,40},{40,48},{48,56},{56,0},{64,72... | collective-permute-start | bytes 786440 | tf_op jit(solution)/shard_map/ppermute | solution.py:293
  183.2 3.6 %collective-permute-start.5 = (bf16[2,2,128,256]{3,2,1,0:T(8,128)(2,1)}, bf16[2,2,128,256]{3,2,1,0:T(8,128)(2,1)}, u32[]{:S(2)}, u32[]{:S(2)}) collective-permute-start(bf16[2,2,128,256]{3,2,1,0:T(8,128)(2,1)} %slice.58), channel_id=1, source_target_pairs={{0,8},{8,16},{16,24},{24,32},{32,40},{40,48},{48,56},{56,0},{64,72... | collective-permute-start | bytes 786440 | tf_op jit(solution)/shard_map/ppermute | solution.py:293
  203.5 3.3 %collective-permute-done.29.refs_18_ = bf16[1,2,128,256]{3,2,1,0:T(8,128)(2,1)S(1)} collective-permute-done((bf16[1,2,128,256]{3,2,1,0:T(8,128)(2,1)S(1)}, bf16[1,2,128,256]{3,2,1,0:T(8,128)(2,1)S(1)}, u32[]{:S(2)}, u32[]{:S(2)}) %collective-permute-start.29) | collective-permute-done | bytes 131104 | tf_op jit(solution)/shard_map/ppermute | solution.py:293
  208.7 13.2 %collective-permute-done.30.refs_19_ = bf16[1,2,128,256]{3,2,1,0:T(8,128)(2,1)S(1)} collective-permute-done((bf16[1,2,128,256]{3,2,1,0:T(8,128)(2,1)S(1)}, bf16[1,2,128,256]{3,2,1,0:T(8,128)(2,1)S(1)}, u32[]{:S(2)}, u32[]{:S(2)}) %collective-permute-start.30) | collective-permute-done | bytes 131104 | tf_op jit(solution)/shard_map/ppermute | solution.py:293
  221.9 4.3 %collective-permute-done.27.refs_17_ = bf16[1,2,128,256]{3,2,1,0:T(8,128)(2,1)S(1)} collective-permute-done((bf16[1,2,128,256]{3,2,1,0:T(8,128)(2,1)S(1)}, bf16[1,2,128,256]{3,2,1,0:T(8,128)(2,1)S(1)}, u32[]{:S(2)}, u32[]{:S(2)}) %collective-permute-start.27) | collective-permute-done | bytes 131104 | tf_op jit(solution)/shard_map/ppermute | solution.py:293
  226.9 16.7 %shard_map.85 = (f32[1024,256]{1,0:T(8,128)}, f32[8,128]{1,0:T(8,128)}) custom-call(s32[54]{0:T(128)} %get-tuple-element.71.code_ref, bf16[1024,512]{1,0:T(8,128)(2,1)} %q_ref.3, f32[1024,512]{1,0:T(8,128)} %refs_2_.1, bf16[8,2,128,256]{3,2,1,0:T(8,128)(2,1)} %bitcast.23, bf16[8,2,128,256]{3,2,1,0:T(8,128)(2,1)} %collective-permute-done.l1_a.refs_1_, ...), custom_call_target="tpu_custom_call" | custom-call | flops 2684354560 | bytes 4194304 | tf_op jit(solution)/shard_map/pallas_call | solution.py:454
  244.7 16.8 %shard_map.87 = (f32[1024,256]{1,0:T(8,128)}, f32[8,128]{1,0:T(8,128)}) custom-call(s32[54]{0:T(128)} %get-tuple-element.70.code_ref, bf16[1024,512]{1,0:T(8,128)(2,1)} %q_ref.3, f32[1024,512]{1,0:T(8,128)} %refs_2_.1, bf16[8,2,128,256]{3,2,1,0:T(8,128)(2,1)} %bitcast.19, bf16[8,2,128,256]{3,2,1,0:T(8,128)(2,1)} %collective-permute-done.7.l1_b.refs_1_, ...), custom_call_target="tpu_custom_call" | custom-call | flops 2684354560 | bytes 4194304 | tf_op jit(solution)/shard_map/pallas_call | solution.py:454
  262.2 33.6 %all_to_all.8 = f32[256,1,128]{2,1,0:T(1,128)} all-to-all(f32[256,1,128]{2,1,0:T(1,128)S(1)} %broadcast_in_dim.75), channel_id=1, replica_groups=mesh['ctx'=32,'head'=8] {'ctx','head'}, dimensions={0} | all-to-all | bytes 262144 | tf_op jit(solution)/shard_map/all_to_all | solution.py:483
  295.8 4.9 %finish.1 = (f32[1024,512]{1,0:T(8,128)}, f32[2]{0:T(128)}) custom-call(f32[256,128]{1,0:T(8,128)} %bitcast.26, f32[1024,256]{1,0:T(8,128)} %get-tuple-element.48.refs_0_, f32[1024,256]{1,0:T(8,128)} %get-tuple-element.49.refs_1_, f32[1024,512]{1,0:T(8,128)} %refs_2_.1), custom_call_target="tpu_custom_call" | custom-call | tf_op jit(solution)/shard_map/finish/pallas_call | solution.py:488
  (169 shorter events, 75.2 us)
Async XLA Ops:
  2.5 29.4 %collective-permute-start = (bf16[8,2,128,256]{3,2,1,0:T(8,128)(2,1)S(1)}, bf16[8,2,128,256]{3,2,1,0:T(8,128)(2,1)}, u32[]{:S(2)}, u32[]{:S(2)}) collective-permute-start(bf16[8,2,128,256]{3,2,1,0:T(8,128)(2,1)S(1)} %bitcast.20), channel_id=1, source_target_pairs={{0,8},{8,16},{16,24},{24,32},{32,40},{40,48},{48,56},{56,0},{64,72... | collective-permute-start | bytes 3145736 | tf_op jit(solution)/shard_map/ppermute | solution.py:293
  5.0 26.9 %collective-permute-start.2 = (bf16[8,2,128,256]{3,2,1,0:T(8,128)(2,1)S(1)}, bf16[8,2,128,256]{3,2,1,0:T(8,128)(2,1)}, u32[]{:S(2)}, u32[]{:S(2)}) collective-permute-start(bf16[8,2,128,256]{3,2,1,0:T(8,128)(2,1)S(1)} %bitcast.21), channel_id=1, source_target_pairs={{0,56},{8,0},{16,8},{24,16},{32,24},{40,32},{48,40},{56,48},{64,12... | collective-permute-start | bytes 3145736 | tf_op jit(solution)/shard_map/ppermute | solution.py:293
  9.1 45.3 %collective-permute-start.7 = (bf16[8,2,128,256]{3,2,1,0:T(8,128)(2,1)S(1)}, bf16[8,2,128,256]{3,2,1,0:T(8,128)(2,1)}, u32[]{:S(2)}, u32[]{:S(2)}) collective-permute-start(bf16[8,2,128,256]{3,2,1,0:T(8,128)(2,1)S(1)} %bitcast.16), channel_id=1, source_target_pairs={{0,8},{8,16},{16,24},{24,32},{32,40},{40,48},{48,56},{56,0},{64,72... | collective-permute-start | bytes 3145736 | tf_op jit(solution)/shard_map/ppermute | solution.py:293
  9.2 45.2 %collective-permute-start.8 = (bf16[8,2,128,256]{3,2,1,0:T(8,128)(2,1)S(1)}, bf16[8,2,128,256]{3,2,1,0:T(8,128)(2,1)}, u32[]{:S(2)}, u32[]{:S(2)}) collective-permute-start(bf16[8,2,128,256]{3,2,1,0:T(8,128)(2,1)S(1)} %bitcast.17), channel_id=1, source_target_pairs={{0,56},{8,0},{16,8},{24,16},{32,24},{40,32},{48,40},{56,48},{64,12... | collective-permute-start | bytes 3145736 | tf_op jit(solution)/shard_map/ppermute | solution.py:293
  27.5 29.5 %collective-permute-start.19 = (bf16[2,2,32,512]{3,2,1,0:T(8,128)(2,1)}, bf16[2,2,32,512]{3,2,1,0:T(8,128)(2,1)S(1)}, u32[]{:S(2)}, u32[]{:S(2)}) collective-permute-start(bf16[2,2,32,512]{3,2,1,0:T(8,128)(2,1)} %get-tuple-element.37), channel_id=1, source_target_pairs={{0,192},{8,200},{16,208},{24,216},{32,224},{40,232},{48,240},{56,2... | collective-permute-start | bytes 393224 | tf_op jit(solution)/shard_map/ppermute | solution.py:293
  31.9 97.4 %collective-permute-start.1 = (bf16[8,2,128,256]{3,2,1,0:T(8,128)(2,1)}, bf16[8,2,128,256]{3,2,1,0:T(8,128)(2,1)S(1)}, u32[]{:S(2)}, u32[]{:S(2)}) collective-permute-start(bf16[8,2,128,256]{3,2,1,0:T(8,128)(2,1)} %collective-permute-done.l1_a.refs_1_), channel_id=1, source_target_pairs={{0,8},{8,16},{16,24},{24,32},{32,40},{40,48},{48,56},{56,0},{64,72... | collective-permute-start | bytes 3145736 | tf_op jit(solution)/shard_map/ppermute | solution.py:293
  31.9 97.4 %collective-permute-start.3 = (bf16[8,2,128,256]{3,2,1,0:T(8,128)(2,1)}, bf16[8,2,128,256]{3,2,1,0:T(8,128)(2,1)S(1)}, u32[]{:S(2)}, u32[]{:S(2)}) collective-permute-start(bf16[8,2,128,256]{3,2,1,0:T(8,128)(2,1)} %collective-permute-done.2.r1_a.refs_7_), channel_id=1, source_target_pairs={{0,56},{8,0},{16,8},{24,16},{32,24},{40,32},{48,40},{56,48},{64,12... | collective-permute-start | bytes 3145736 | tf_op jit(solution)/shard_map/ppermute | solution.py:293
  54.4 75.0 %collective-permute-start.15 = (bf16[8,2,128,256]{3,2,1,0:T(8,128)(2,1)}, bf16[8,2,128,256]{3,2,1,0:T(8,128)(2,1)}, u32[]{:S(2)}, u32[]{:S(2)}) collective-permute-start(bf16[8,2,128,256]{3,2,1,0:T(8,128)(2,1)} %collective-permute-done.7.l1_b.refs_1_), channel_id=1, source_target_pairs={{0,8},{8,16},{16,24},{24,32},{32,40},{40,48},{48,56},{56,0},{64,72... | collective-permute-start | bytes 3145736 | tf_op jit(solution)/shard_map/ppermute | solution.py:293
  54.4 75.0 %collective-permute-start.16 = (bf16[8,2,128,256]{3,2,1,0:T(8,128)(2,1)}, bf16[8,2,128,256]{3,2,1,0:T(8,128)(2,1)}, u32[]{:S(2)}, u32[]{:S(2)}) collective-permute-start(bf16[8,2,128,256]{3,2,1,0:T(8,128)(2,1)} %collective-permute-done.8.r1_b.refs_7_), channel_id=1, source_target_pairs={{0,56},{8,0},{16,8},{24,16},{32,24},{40,32},{48,40},{56,48},{64,12... | collective-permute-start | bytes 3145736 | tf_op jit(solution)/shard_map/ppermute | solution.py:293
  59.9 42.1 %collective-permute-start.20 = (bf16[2,2,32,512]{3,2,1,0:T(8,128)(2,1)}, bf16[2,2,32,512]{3,2,1,0:T(8,128)(2,1)S(1)}, u32[]{:S(2)}, u32[]{:S(2)}) collective-permute-start(bf16[2,2,32,512]{3,2,1,0:T(8,128)(2,1)} %shard_map.81.refs_0_.refs_2_.refs_3_.refs_4_.refs_5_.refs_6_), channel_id=1, source_target_pairs={{0,8},{8,16},{16,24},{24,32},{32,40},{40,48},{48,56},{56,0},{64,72... | collective-permute-start | bytes 393224 | tf_op jit(solution)/shard_map/ppermute | solution.py:293
  124.2 22.0 %collective-permute-start.11 = (bf16[6,2,128,256]{3,2,1,0:T(8,128)(2,1)}, bf16[6,2,128,256]{3,2,1,0:T(8,128)(2,1)}, u32[]{:S(2)}, u32[]{:S(2)}) collective-permute-start(bf16[6,2,128,256]{3,2,1,0:T(8,128)(2,1)} %get-tuple-element.30), channel_id=1, source_target_pairs={{0,128},{8,136},{16,144},{24,152},{32,160},{40,168},{48,176},{56,1... | collective-permute-start | bytes 2359304 | tf_op jit(solution)/shard_map/ppermute | solution.py:293
  135.5 16.3 %collective-permute-start.31 = (bf16[6,2,128,256]{3,2,1,0:T(8,128)(2,1)}, bf16[6,2,128,256]{3,2,1,0:T(8,128)(2,1)S(1)}, u32[]{:S(2)}, u32[]{:S(2)}) collective-permute-start(bf16[6,2,128,256]{3,2,1,0:T(8,128)(2,1)} %get-tuple-element.42), channel_id=1, source_target_pairs={{0,8},{8,16},{16,24},{24,32},{32,40},{40,48},{48,56},{56,0},{64,72... | collective-permute-start | bytes 2359304 | tf_op jit(solution)/shard_map/ppermute | solution.py:293
  140.2 14.7 %collective-permute-start.33 = (bf16[6,2,128,256]{3,2,1,0:T(8,128)(2,1)}, bf16[6,2,128,256]{3,2,1,0:T(8,128)(2,1)S(1)}, u32[]{:S(2)}, u32[]{:S(2)}) collective-permute-start(bf16[6,2,128,256]{3,2,1,0:T(8,128)(2,1)} %get-tuple-element.43), channel_id=1, source_target_pairs={{0,56},{8,0},{16,8},{24,16},{32,24},{40,32},{48,40},{56,48},{64,12... | collective-permute-start | bytes 2359304 | tf_op jit(solution)/shard_map/ppermute | solution.py:293
  143.6 28.2 %collective-permute-start.6 = (bf16[6,2,128,256]{3,2,1,0:T(8,128)(2,1)}, bf16[6,2,128,256]{3,2,1,0:T(8,128)(2,1)S(1)}, u32[]{:S(2)}, u32[]{:S(2)}) collective-permute-start(bf16[6,2,128,256]{3,2,1,0:T(8,128)(2,1)} %get-tuple-element.27), channel_id=1, source_target_pairs={{0,56},{8,0},{16,8},{24,16},{32,24},{40,32},{48,40},{56,48},{64,12... | collective-permute-start | bytes 2359304 | tf_op jit(solution)/shard_map/ppermute | solution.py:293
  145.4 30.1 %collective-permute-start.10 = (bf16[8,2,128,256]{3,2,1,0:T(8,128)(2,1)}, bf16[8,2,128,256]{3,2,1,0:T(8,128)(2,1)}, u32[]{:S(2)}, u32[]{:S(2)}) collective-permute-start(bf16[8,2,128,256]{3,2,1,0:T(8,128)(2,1)} %get-tuple-element.29), channel_id=1, source_target_pairs={{0,192},{8,200},{16,208},{24,216},{32,224},{40,232},{48,240},{56,2... | collective-permute-start | bytes 3145736 | tf_op jit(solution)/shard_map/ppermute | solution.py:293
  146.2 32.4 %collective-permute-start.9 = (bf16[8,2,128,256]{3,2,1,0:T(8,128)(2,1)}, bf16[8,2,128,256]{3,2,1,0:T(8,128)(2,1)}, u32[]{:S(2)}, u32[]{:S(2)}) collective-permute-start(bf16[8,2,128,256]{3,2,1,0:T(8,128)(2,1)} %get-tuple-element.28), channel_id=1, source_target_pairs={{0,64},{8,72},{16,80},{24,88},{32,96},{40,104},{48,112},{56,120},{... | collective-permute-start | bytes 3145736 | tf_op jit(solution)/shard_map/ppermute | solution.py:293
  151.8 28.7 %collective-permute-start.24 = (bf16[5,2,128,256]{3,2,1,0:T(8,128)(2,1)}, bf16[5,2,128,256]{3,2,1,0:T(8,128)(2,1)}, u32[]{:S(2)}, u32[]{:S(2)}) collective-permute-start(bf16[5,2,128,256]{3,2,1,0:T(8,128)(2,1)} %get-tuple-element.38), channel_id=1, source_target_pairs={{0,64},{8,72},{16,80},{24,88},{32,96},{40,104},{48,112},{56,120},{... | collective-permute-start | bytes 1966088 | tf_op jit(solution)/shard_map/ppermute | solution.py:293
  154.9 26.7 %collective-permute-start.4 = (bf16[6,2,128,256]{3,2,1,0:T(8,128)(2,1)}, bf16[6,2,128,256]{3,2,1,0:T(8,128)(2,1)S(1)}, u32[]{:S(2)}, u32[]{:S(2)}) collective-permute-start(bf16[6,2,128,256]{3,2,1,0:T(8,128)(2,1)} %get-tuple-element.26), channel_id=1, source_target_pairs={{0,8},{8,16},{16,24},{24,32},{32,40},{40,48},{48,56},{56,0},{64,72... | collective-permute-start | bytes 2359304 | tf_op jit(solution)/shard_map/ppermute | solution.py:293
  181.6 16.1 %collective-permute-start.26 = (bf16[5,2,128,256]{3,2,1,0:T(8,128)(2,1)}, bf16[5,2,128,256]{3,2,1,0:T(8,128)(2,1)}, u32[]{:S(2)}, u32[]{:S(2)}) collective-permute-start(bf16[5,2,128,256]{3,2,1,0:T(8,128)(2,1)} %get-tuple-element.40), channel_id=1, source_target_pairs={{0,128},{8,136},{16,144},{24,152},{32,160},{40,168},{48,176},{56,1... | collective-permute-start | bytes 1966088 | tf_op jit(solution)/shard_map/ppermute | solution.py:293
  197.8 45.9 %collective-permute-start.35 = (bf16[3,2,128,256]{3,2,1,0:T(8,128)(2,1)}, bf16[3,2,128,256]{3,2,1,0:T(8,128)(2,1)S(1)}, u32[]{:S(2)}, u32[]{:S(2)}) collective-permute-start(bf16[3,2,128,256]{3,2,1,0:T(8,128)(2,1)} %get-tuple-element.44), channel_id=1, source_target_pairs={{0,64},{8,72},{16,80},{24,88},{32,96},{40,104},{48,112},{56,120},{... | collective-permute-start | bytes 1179656 | tf_op jit(solution)/shard_map/ppermute | solution.py:293
  199.2 44.5 %collective-permute-start.36 = (bf16[3,2,128,256]{3,2,1,0:T(8,128)(2,1)}, bf16[3,2,128,256]{3,2,1,0:T(8,128)(2,1)S(1)}, u32[]{:S(2)}, u32[]{:S(2)}) collective-permute-start(bf16[3,2,128,256]{3,2,1,0:T(8,128)(2,1)} %get-tuple-element.45), channel_id=1, source_target_pairs={{0,192},{8,200},{16,208},{24,216},{32,224},{40,232},{48,240},{56,2... | collective-permute-start | bytes 1179656 | tf_op jit(solution)/shard_map/ppermute | solution.py:293
  200.6 43.1 %collective-permute-start.37 = (bf16[3,2,128,256]{3,2,1,0:T(8,128)(2,1)}, bf16[3,2,128,256]{3,2,1,0:T(8,128)(2,1)S(1)}, u32[]{:S(2)}, u32[]{:S(2)}) collective-permute-start(bf16[3,2,128,256]{3,2,1,0:T(8,128)(2,1)} %get-tuple-element.46), channel_id=1, source_target_pairs={{0,128},{8,136},{16,144},{24,152},{32,160},{40,168},{48,176},{56,1... | collective-permute-start | bytes 1179656 | tf_op jit(solution)/shard_map/ppermute | solution.py:293
  200.9 21.0 %collective-permute-start.30 = (bf16[1,2,128,256]{3,2,1,0:T(8,128)(2,1)S(1)}, bf16[1,2,128,256]{3,2,1,0:T(8,128)(2,1)S(1)}, u32[]{:S(2)}, u32[]{:S(2)}) collective-permute-start(bf16[1,2,128,256]{3,2,1,0:T(8,128)(2,1)S(1)} %get-tuple-element.61), channel_id=1, source_target_pairs={{0,128},{8,136},{16,144},{24,152},{32,160},{40,168},{48,176},{56,1... | collective-permute-start | bytes 393224 | tf_op jit(solution)/shard_map/ppermute | solution.py:293
  206.8 19.4 %collective-permute-start.27 = (bf16[1,2,128,256]{3,2,1,0:T(8,128)(2,1)S(1)}, bf16[1,2,128,256]{3,2,1,0:T(8,128)(2,1)S(1)}, u32[]{:S(2)}, u32[]{:S(2)}) collective-permute-start(bf16[1,2,128,256]{3,2,1,0:T(8,128)(2,1)S(1)} %slice.60), channel_id=1, source_target_pairs={{0,64},{8,72},{16,80},{24,88},{32,96},{40,104},{48,112},{56,120},{... | collective-permute-start | bytes 393224 | tf_op jit(solution)/shard_map/ppermute | solution.py:293
  (45 other events, 603.3 us)

commit v3 on v2

--- a/solution.py
+++ b/solution.py
@@ -65,16 +65,24 @@
 def start_choice(arrays, ids, code, dst, sem):
     which = lax.shift_right_logical(code, 3)
     slot = code & 7
-    for k in ids:
-        @pl.when(which == k)
-        def _(k=k):
-            pltpu.make_async_copy(arrays[k].at[slot], dst, sem).start()
+
+    def search(options):
+        if len(options) == 1:
+            pltpu.make_async_copy(arrays[options[0]].at[slot], dst, sem).start()
+            return
+        half = len(options) // 2
+        lax.cond(
+            which < options[half], lambda: search(options[:half]), lambda: search(options[half:])
+        )
+
+    search(sorted(ids))
 
 
 def attention_kernel(nblocks, chunk, narrays, code_ref, q_ref, vec_ref, *refs):
     arrays = refs[:narrays]
     quarter = refs[narrays]
-    out_ref, stat_ref, kvbuf, sems, acc = refs[narrays + 1 :]
+    before = refs[narrays + 1 : -5]
+    out_ref, stat_ref, kvbuf, sems, acc = refs[-5:]
     b = pl.program_id(0)
     width = q_ref.shape[1]
     table = nblocks * 6
@@ -95,7 +103,7 @@
                 if array is None:
                     src = quarter.at[g, :, :, cols]
                 else:
-                    src = arrays[array].at[4, :, pl.ds((2 * g + chunk[1]) * part, part)]
+                    src = arrays[array].at[2, :, pl.ds((2 * g + chunk[1]) * part, part)]
                 copies.append(pltpu.make_async_copy(src, dst, sem))
         return copies
 
@@ -154,8 +162,11 @@
     @pl.when(b == nblocks - 1)
     def _():
         s, c, r = combine(acc[:, 0, :], acc[:, 1, :], acc[:, 2, :])
-        lane = lax.broadcasted_iota(jnp.int32, stat_ref.shape, 1) - 3 * chunk[1]
-        stat_ref[...] = jnp.where(lane == 0, s, jnp.where(lane == 1, c, jnp.where(lane == 2, r, 0.0)))
+        lane = lax.broadcasted_iota(jnp.int32, (1, BS), 1) - 3 * chunk[1]
+        row = jnp.where(lane == 0, s, jnp.where(lane == 1, c, jnp.where(lane == 2, r, 0.0)))
+        for ref in before:
+            row = row + ref[0:1, :]
+        stat_ref[...] = jnp.broadcast_to(row, stat_ref.shape)
 
 
 def run_copies(plan, sems):
@@ -177,39 +188,37 @@
     run_copies(plan, sems)
 
 
-def third_hop(pick_ref, l2, r2, plus, minus):
+def third_kernel(pick_ref, l2, r2, plus, minus, sems):
     plan = []
     for i in range(6):
         plan.append((l2.at[pick_ref[i]], plus.at[i]))
         plan.append((r2.at[pick_ref[6 + i]], minus.at[i]))
-    return plan
-
-
-def third_kernel(pick_ref, l2, r2, plus, minus, sems):
-    run_copies(third_hop(pick_ref, l2, r2, plus, minus), sems)
-
-
-def second_kernel(pick_ref, l2_a, r2_a, l2_b, r2_b, quarter, plus, minus, yp, y2, ym, sems):
-    plan = third_hop(pick_ref, l2_b, r2_b, plus, minus)
+    run_copies(plan, sems)
+
+
+def second_kernel(pick_ref, l2, r2, quarter, yp, y2, ym, sems):
+    plan = []
+    part, half = quarter.shape[2], quarter.shape[3] // 2
     for row, out in enumerate((yp, y2, ym)):
-        for i, src in enumerate((l2_a, r2_a, l2_b, r2_b)):
-            plan.append((src.at[pick_ref[12 + row * 5 + 3 + i % 2]], out.at[i]))
-        part, half = quarter.shape[2], quarter.shape[3] // 2
+        for i, src in enumerate((l2, r2)):
+            plan.append((src.at[pick_ref[12 + row * 5 + 3 + i]], out.at[i]))
         for g in range(2):
             for k in range(2):
                 plan.append(
                     (
                         quarter.at[g, :, :, pl.ds(k * half, half)],
-                        out.at[4, :, pl.ds((2 * g + k) * part, part)],
+                        out.at[2, :, pl.ds((2 * g + k) * part, part)],
                     )
                 )
     run_copies(plan, sems)
 
 
-def half_kernel(a3, b3, yp, y2, ym, sems):
+def half_kernel(pick_ref, a3, b3, l2, r2, yp, y2, ym, sems):
     plan = []
     for row, out in enumerate((yp, y2, ym)):
         plan += [(a3.at[row + 1], out.at[0]), (b3.at[row + 1], out.at[1])]
+        for i, src in enumerate((l2, r2)):
+            plan.append((src.at[pick_ref[12 + row * 5 + 3 + i]], out.at[2 + i]))
     run_copies(plan, sems)
 
 
@@ -358,8 +367,8 @@
     codes = []
     for chunk in range(2):
         edge_slot = chunk * 4 + 3
-        far = jnp.where(late, LYP, jnp.where(second, MP, YP)) + row
-        base = jnp.where(late, 0, jnp.where(second, chunk * 2 - 3, chunk * jnp.where(row == 2, 3, 4)))
+        far = jnp.where(late, LYP, jnp.where(second, FP if chunk else MP, YP)) + row
+        base = jnp.where(late, 0, jnp.where(second, 2 * chunk - 3, chunk * jnp.where(row == 2, 3, 4)))
         if chunk == 0:
             far = jnp.where(dz == 4, FP + row, far)
             base = jnp.where(dz == 4, -2, base)
@@ -427,15 +436,12 @@
     )
     plus, minus = pack(third_kernel, picks, (l2[0], r2[0]), (slots(6), slots(6)), 12)
     a3, b3 = send(plus, z_shift(1)), send(minus, z_shift(-1))
-    plus, minus, *two = pack(
-        second_kernel, picks, (l2[0], r2[0], l2[1], r2[1], quarter),
-        (slots(6), slots(6)) + (slots(5),) * 3, 36,
-    )
-    y2 = rows_of(two)
+    y2 = rows_of(pack(second_kernel, picks, (l2[0], r2[0], quarter), (slots(3),) * 3, 18))
+    plus, minus = pack(third_kernel, picks, (l2[1], r2[1]), (slots(6), slots(6)), 12)
     c3, d3 = send(plus, z_shift(1)), send(minus, z_shift(-1))
     a4, b4 = send(a3[4:6], z_shift(1)), send(b3[4:6], z_shift(-1))
     c4, d4 = send(c3[4:6], z_shift(1)), send(d3[4:6], z_shift(-1))
-    y3a = rows_of(pack(half_kernel, None, (a3, b3), (slots(2),) * 3, 6))
+    y3a = rows_of(pack(half_kernel, picks, (a3, b3, l2[1], r2[1]), (slots(4),) * 3, 12))
     y4a = rows_of((a4[1:2], b4[0:1], b4[1:2]))
     y3b = rows_of(pack(late_kernel, None, (c3, d3, c4, d4), (slots(3),) * 3, 9))
 
@@ -445,26 +451,29 @@
     sources = (
         (own[0], l1[0], l2[0], a3, a4, b3, r2[0], r1[0]) + by_code(y1) + by_code(y3a) + by_code(y2)
         + by_code(y4a),
-        (own[1], l1[1], l2[1], c3, c4, d3, r2[1], r1[1]) + by_code(y1) + by_code(y3b) + by_code(y2),
+        (own[1], l1[1], l2[1], c3, c4, d3, r2[1], r1[1]) + by_code(y1) + by_code(y3b) + by_code(y2)
+        + by_code(y3a),
     )
     products = []
     stats = []
     keys = LIST * BS
     for k, arrays in enumerate(sources):
+        stat_rows = 8 if k + 1 < len(sources) else nctx * nhead
         product, stat = pl.pallas_call(
             functools.partial(attention_kernel, nblocks, (CHUNKS[k][0], k), len(arrays)),
             out_shape=(
                 jax.ShapeDtypeStruct((rows, cw), jnp.float32),
-                jax.ShapeDtypeStruct((8, 128), jnp.float32),
+                jax.ShapeDtypeStruct((stat_rows, BS), jnp.float32),
             ),
             grid_spec=pltpu.PrefetchScalarGridSpec(
                 num_scalar_prefetch=1,
                 grid=(nblocks,),
                 in_specs=[pl.BlockSpec((BS, cw), lambda b, *_, k=k: (b, k))] * 2
-                + [ANY] * (len(arrays) + 1),
+                + [ANY] * (len(arrays) + 1)
+                + [pl.BlockSpec((8, BS), lambda b, *_: (0, 0))] * len(stats),
                 out_specs=(
                     pl.BlockSpec((BS, cw), lambda b, *_: (b, 0)),
-                    pl.BlockSpec((8, 128), lambda b, *_: (0, 0)),
+                    pl.BlockSpec((stat_rows, BS), lambda b, *_: (0, 0)),
                 ),
                 scratch_shapes=[
                     pltpu.VMEM((2, 2, keys, cw), jnp.bfloat16),
@@ -476,11 +485,10 @@
                 flops=10 * rows * keys * cw, bytes_accessed=16 * rows * cw,
                 transcendentals=rows * keys * (cw // HD),
             ),
-        )(codes[k], queries, lanczos_vec, *arrays, quarter)
+        )(codes[k], queries, lanczos_vec, *arrays, quarter, *stats)
         products.append(product)
-        stats.append(stat)
-    sent = jnp.broadcast_to(sum(stats)[:1], (nctx * nhead, 128))
-    gathered = lax.all_to_all(sent, ("ctx", "head"), 0, 0, tiled=True)
+        stats = [stat]
+    gathered = lax.all_to_all(stats[0], ("ctx", "head"), 0, 0, tiled=True)
     count = float(rows * width * nctx * nhead)
     step = rows // 4
     fin_spec = pl.BlockSpec((step, width), lambda i: (i, 0))

time: 301 us -> 299 us (level)
  waiting for transfers between devices: 128 us -> 103 us
  starting transfers between devices: 58 us -> 72 us
  local copies, waits for them, and re-layouts: 13.3 us -> 20.1 us
  blocking collectives: 33.6 us -> 28.1 us
  other arithmetic: 1.74 us -> 6.1 us
  Pallas kernels: 64.8 us -> 67.9 us
    ppermute x38, waiting for transfers between devices: 128 us -> 103 us  [send(): return lax.ppermute(x, 'ctx', pairs)]
    ppermute x38, starting transfers between devices: 58 us -> 72 us  [send(): return lax.ppermute(x, 'ctx', pairs)]
    all_to_all x1, blocking collectives: 33.6 us -> 28.1 us  [whole_step(): gathered = lax.all_to_all(stats[0], ('ctx', 'head'), 0, 0, tiled=True)]
    pallas_call x9 -> x10, Pallas kernels: 26.4 us -> 29.2 us  [pack(): pl.pallas_call(kernel, out_shape=tuple((jax.ShapeDtypeStruct(shape, jnp.b...]
  transfers between devices with their start and end apart: 38 -> 38, of which waited for: 16 -> 11; matrix products, arithmetic and copies ran while one was open for 3% -> 7% of each run, Pallas kernels for 14% -> 15%
where the time goes in v3:
time: 299 us; the launch traced here: 298 us
  waiting for transfers between devices  103 us (34%)
  starting transfers between devices  72 us (24%)
  Pallas kernels  67.9 us (23%)
  blocking collectives  28.1 us (9%)
  local copies, waits for them, and re-layouts  20.1 us (7%)
  other arithmetic  6.1 us (2%)
    ppermute x38, waiting for transfers between devices, send(): return lax.ppermute(x, 'ctx', pairs)  103 us
    ppermute x38, starting transfers between devices, send(): return lax.ppermute(x, 'ctx', pairs)  72 us
    pallas_call x2, Pallas kernels, whole_step(): pl.pallas_call(functools.partial(attention_kernel, nblocks, (CHUNKS[k][0]...  33.8 us
    pallas_call x10, Pallas kernels, pack(): pl.pallas_call(kernel, out_shape=tuple((jax.ShapeDtypeStruct(shape, jnp.b...  29.2 us
    all_to_all x1, blocking collectives, whole_step(): gathered = lax.all_to_all(stats[0], ('ctx', 'head'), 0, 0, tiled=True)  28.1 us
  transfers between devices with their start and end apart: 38, of which 11 were waited for; matrix products, arithmetic and copies ran while one was open for 7% of the time, Pallas kernels for 15%

profile of v3, /device:TPU:1, one launch (start us, length us, event | category | flops | bytes accessed | tf_op | source)
XLA Modules:
  0.0 298.4 jit_solution(6319863111738794086)
XLA Ops:
  5.0 4.0 %collective-permute-start.8 = (bf16[8,2,128,256]{3,2,1,0:T(8,128)(2,1)S(1)}, bf16[8,2,128,256]{3,2,1,0:T(8,128)(2,1)}, u32[]{:S(2)}, u32[]{:S(2)}) collective-permute-start(bf16[8,2,128,256]{3,2,1,0:T(8,128)(2,1)S(1)} %bitcast.22), channel_id=1, source_target_pairs={{0,56},{8,0},{16,8},{24,16},{32,24},{40,32},{48,40},{56,48},{64,12... | collective-permute-start | bytes 3145736 | tf_op jit(solution)/shard_map/ppermute | solution.py:302
  12.9 19.0 %collective-permute-done.7.l1_a.refs_1_ = bf16[8,2,128,256]{3,2,1,0:T(8,128)(2,1)} collective-permute-done((bf16[8,2,128,256]{3,2,1,0:T(8,128)(2,1)S(1)}, bf16[8,2,128,256]{3,2,1,0:T(8,128)(2,1)}, u32[]{:S(2)}, u32[]{:S(2)}) %collective-permute-start.7) | collective-permute-done | bytes 1048608 | tf_op jit(solution)/shard_map/ppermute | solution.py:302
  36.6 4.4 %collective-permute-done.18.refs_1_ = bf16[2,2,32,512]{3,2,1,0:T(8,128)(2,1)S(1)} collective-permute-done((bf16[2,2,32,512]{3,2,1,0:T(8,128)(2,1)}, bf16[2,2,32,512]{3,2,1,0:T(8,128)(2,1)S(1)}, u32[]{:S(2)}, u32[]{:S(2)}) %collective-permute-start.18) | collective-permute-done | bytes 131104 | tf_op jit(solution)/shard_map/ppermute | solution.py:302
  42.6 3.9 %collective-permute-done.19.refs_2_ = bf16[2,2,32,512]{3,2,1,0:T(8,128)(2,1)S(1)} collective-permute-done((bf16[2,2,32,512]{3,2,1,0:T(8,128)(2,1)}, bf16[2,2,32,512]{3,2,1,0:T(8,128)(2,1)S(1)}, u32[]{:S(2)}, u32[]{:S(2)}) %collective-permute-start.19) | collective-permute-done | bytes 131104 | tf_op jit(solution)/shard_map/ppermute | solution.py:302
  48.0 3.0 collective-permute-done.20.refs_3_
  53.9 25.6 %collective-permute-done.21.refs_1_ = bf16[2,2,32,512]{3,2,1,0:T(8,128)(2,1)S(1)} collective-permute-done((bf16[2,2,32,512]{3,2,1,0:T(8,128)(2,1)}, bf16[2,2,32,512]{3,2,1,0:T(8,128)(2,1)S(1)}, u32[]{:S(2)}, u32[]{:S(2)}) %collective-permute-start.21) | collective-permute-done | bytes 131104 | tf_op jit(solution)/shard_map/ppermute | solution.py:302
  89.1 4.3 %shard_map.78 = (bf16[8,2,128,256]{3,2,1,0:T(8,128)(2,1)}, bf16[6,2,128,256]{3,2,1,0:T(8,128)(2,1)}, bf16[8,2,128,256]{3,2,1,0:T(8,128)(2,1)}) custom-call(s32[37]{0:T(128)} %concatenate.17.pick_ref, bf16[8,2,128,256]{3,2,1,0:T(8,128)(2,1)} %bitcast.23, bf16[8,2,128,256]{3,2,1,0:T(8,128)(2,1)} %collective-permute-done.7.l1_a.refs_1_, ...), custom_call_target="tpu_custom_call" | custom-call | bytes 6000000 | tf_op jit(solution)/shard_map/pallas_call | solution.py:310
  93.4 17.6 %collective-permute-done.23.refs_2_.refs_3_.refs_4_ = bf16[2,2,32,512]{3,2,1,0:T(8,128)(2,1)S(1)} collective-permute-done((bf16[2,2,32,512]{3,2,1,0:T(8,128)(2,1)}, bf16[2,2,32,512]{3,2,1,0:T(8,128)(2,1)S(1)}, u32[]{:S(2)}, u32[]{:S(2)}) %collective-permute-start.23) | collective-permute-done | bytes 131104 | tf_op jit(solution)/shard_map/ppermute | solution.py:302
  115.9 3.4 %shard_map.85 = (bf16[6,2,128,256]{3,2,1,0:T(8,128)(2,1)}, bf16[6,2,128,256]{3,2,1,0:T(8,128)(2,1)}) custom-call(s32[37]{0:T(128)} %concatenate.17.pick_ref, bf16[8,2,128,256]{3,2,1,0:T(8,128)(2,1)} %copy-done.2, bf16[8,2,128,256]{3,2,1,0:T(8,128)(2,1)} %copy-done.3), custom_call_target="tpu_custom_call" | custom-call | bytes 6000000 | tf_op jit(solution)/shard_map/pallas_call | solution.py:310
  119.3 3.8 %collective-permute-start.28 = (bf16[6,2,128,256]{3,2,1,0:T(8,128)(2,1)}, bf16[6,2,128,256]{3,2,1,0:T(8,128)(2,1)S(1)}, u32[]{:S(2)}, u32[]{:S(2)}) collective-permute-start(bf16[6,2,128,256]{3,2,1,0:T(8,128)(2,1)} %get-tuple-element.41), channel_id=1, source_target_pairs={{0,8},{8,16},{16,24},{24,32},{32,40},{40,48},{48,56},{56,0},{64,72... | collective-permute-start | bytes 2359304 | tf_op jit(solution)/shard_map/ppermute | solution.py:302
  123.1 8.6 %collective-permute-done.3.r2.refs_6_ = bf16[8,2,128,256]{3,2,1,0:T(8,128)(2,1)} collective-permute-done((bf16[8,2,128,256]{3,2,1,0:T(8,128)(2,1)}, bf16[8,2,128,256]{3,2,1,0:T(8,128)(2,1)}, u32[]{:S(2)}, u32[]{:S(2)}) %collective-permute-start.3) | collective-permute-done | bytes 1048608 | tf_op jit(solution)/shard_map/ppermute | solution.py:302
  131.7 3.4 %shard_map.77 = (bf16[6,2,128,256]{3,2,1,0:T(8,128)(2,1)}, bf16[6,2,128,256]{3,2,1,0:T(8,128)(2,1)}) custom-call(s32[37]{0:T(128)} %concatenate.17.pick_ref, bf16[8,2,128,256]{3,2,1,0:T(8,128)(2,1)} %collective-permute-done.1.l2.refs_2_, bf16[8,2,128,256]{3,2,1,0:T(8,128)(2,1)} %collective-permute-done.3.r2.refs_6_), custom_call_target="tpu_custom_call" | custom-call | bytes 6000000 | tf_op jit(solution)/shard_map/pallas_call | solution.py:310
  135.2 14.7 %collective-permute-start.9 = (bf16[8,2,128,256]{3,2,1,0:T(8,128)(2,1)}, bf16[8,2,128,256]{3,2,1,0:T(8,128)(2,1)}, u32[]{:S(2)}, u32[]{:S(2)}) collective-permute-start(bf16[8,2,128,256]{3,2,1,0:T(8,128)(2,1)} %get-tuple-element.28), channel_id=1, source_target_pairs={{0,64},{8,72},{16,80},{24,88},{32,96},{40,104},{48,112},{56,120},{... | collective-permute-start | bytes 3145736 | tf_op jit(solution)/shard_map/ppermute | solution.py:302
  152.4 3.1 %shard_map.84 = (bf16[3,2,128,256]{3,2,1,0:T(8,128)(2,1)}, bf16[3,2,128,256]{3,2,1,0:T(8,128)(2,1)}, bf16[3,2,128,256]{3,2,1,0:T(8,128)(2,1)}) custom-call(s32[37]{0:T(128)} %concatenate.17.pick_ref, bf16[8,2,128,256]{3,2,1,0:T(8,128)(2,1)} %copy-done.2, bf16[8,2,128,256]{3,2,1,0:T(8,128)(2,1)} %copy-done.3, bf16[2,2,32,512]{3,2,1,0:T(8,128)(2,1)} %shard_map.83.quarter.refs_20_), custom_call_target="tpu_custom_call" | custom-call | bytes 6000000 | tf_op jit(solution)/shard_map/pallas_call | solution.py:310
  159.7 10.2 %collective-permute-done.6.b3.refs_5_ = bf16[6,2,128,256]{3,2,1,0:T(8,128)(2,1)S(1)} collective-permute-done((bf16[6,2,128,256]{3,2,1,0:T(8,128)(2,1)}, bf16[6,2,128,256]{3,2,1,0:T(8,128)(2,1)S(1)}, u32[]{:S(2)}, u32[]{:S(2)}) %collective-permute-start.6) | collective-permute-done | bytes 786464 | tf_op jit(solution)/shard_map/ppermute | solution.py:302
  169.8 3.4 %collective-permute-start.35 = (bf16[2,2,128,256]{3,2,1,0:T(8,128)(2,1)}, bf16[2,2,128,256]{3,2,1,0:T(8,128)(2,1)}, u32[]{:S(2)}, u32[]{:S(2)}) collective-permute-start(bf16[2,2,128,256]{3,2,1,0:T(8,128)(2,1)} %slice.56), channel_id=1, source_target_pairs={{0,56},{8,0},{16,8},{24,16},{32,24},{40,32},{48,40},{56,48},{64,12... | collective-permute-start | bytes 786440 | tf_op jit(solution)/shard_map/ppermute | solution.py:302
  183.3 2.8 collective-permute-start.27
  187.4 3.4 %shard_map.86 = (bf16[4,2,128,256]{3,2,1,0:T(8,128)(2,1)}, bf16[4,2,128,256]{3,2,1,0:T(8,128)(2,1)}, bf16[4,2,128,256]{3,2,1,0:T(8,128)(2,1)}) custom-call(s32[37]{0:T(128)} %concatenate.17.pick_ref, bf16[6,2,128,256]{3,2,1,0:T(8,128)(2,1)} %copy-done.6, bf16[6,2,128,256]{3,2,1,0:T(8,128)(2,1)} %copy-done.7, ...), custom_call_target="tpu_custom_call" | custom-call | bytes 6000000 | tf_op jit(solution)/shard_map/pallas_call | solution.py:310
  210.9 7.7 %collective-permute-done.37.refs_19_ = bf16[1,2,128,256]{3,2,1,0:T(8,128)(2,1)S(1)} collective-permute-done((bf16[1,2,128,256]{3,2,1,0:T(8,128)(2,1)}, bf16[1,2,128,256]{3,2,1,0:T(8,128)(2,1)S(1)}, u32[]{:S(2)}, u32[]{:S(2)}) %collective-permute-start.37) | collective-permute-done | bytes 131104 | tf_op jit(solution)/shard_map/ppermute | solution.py:302
  218.6 6.1 %collective-permute-start.13 = (bf16[3,2,128,256]{3,2,1,0:T(8,128)(2,1)}, bf16[3,2,128,256]{3,2,1,0:T(8,128)(2,1)S(1)}, u32[]{:S(2)}, u32[]{:S(2)}) collective-permute-start(bf16[3,2,128,256]{3,2,1,0:T(8,128)(2,1)} %get-tuple-element.31), channel_id=1, source_target_pairs={{0,64},{8,72},{16,80},{24,88},{32,96},{40,104},{48,112},{56,120},{... | collective-permute-start | bytes 1179656 | tf_op jit(solution)/shard_map/ppermute | solution.py:302
  230.7 16.9 %shard_map.87 = (f32[1024,256]{1,0:T(8,128)}, f32[8,128]{1,0:T(8,128)}) custom-call(s32[54]{0:T(128)} %get-tuple-element.70.code_ref, bf16[1024,512]{1,0:T(8,128)(2,1)} %q_ref.3, f32[1024,512]{1,0:T(8,128)} %refs_2_.1, bf16[8,2,128,256]{3,2,1,0:T(8,128)(2,1)} %bitcast.24, bf16[8,2,128,256]{3,2,1,0:T(8,128)(2,1)} %collective-permute-done.7.l1_a.refs_1_, ...), custom_call_target="tpu_custom_call" | custom-call | flops 2684354560 | bytes 4194304 | tf_op jit(solution)/shard_map/pallas_call | solution.py:462
  248.5 17.0 %shard_map.88 = (f32[1024,256]{1,0:T(8,128)}, f32[256,128]{1,0:T(8,128)}) custom-call(s32[54]{0:T(128)} %get-tuple-element.71.code_ref, bf16[1024,512]{1,0:T(8,128)(2,1)} %q_ref.3, f32[1024,512]{1,0:T(8,128)} %refs_2_.1, bf16[8,2,128,256]{3,2,1,0:T(8,128)(2,1)} %bitcast.20, bf16[8,2,128,256]{3,2,1,0:T(8,128)(2,1)} %collective-permute-done.l1_b.refs_1_, ...), custom_call_target="tpu_custom_call" | custom-call | flops 2684354560 | bytes 4194304 | tf_op jit(solution)/shard_map/pallas_call | solution.py:462
  265.4 28.1 %all_to_all.11 = f32[256,1,128]{2,1,0:T(1,128)} all-to-all(f32[256,1,128]{2,1,0:T(1,128)} %bitcast.28), channel_id=1, replica_groups=mesh['ctx'=32,'head'=8] {'ctx','head'}, dimensions={0} | all-to-all | bytes 262144 | tf_op jit(solution)/shard_map/all_to_all | solution.py:491
  293.5 4.9 %finish.1 = (f32[1024,512]{1,0:T(8,128)}, f32[2]{0:T(128)}) custom-call(f32[256,128]{1,0:T(8,128)} %bitcast.27, f32[1024,256]{1,0:T(8,128)} %get-tuple-element.48.refs_0_, f32[1024,256]{1,0:T(8,128)} %get-tuple-element.49.refs_1_, f32[1024,512]{1,0:T(8,128)} %refs_2_.1), custom_call_target="tpu_custom_call" | custom-call | tf_op jit(solution)/shard_map/finish/pallas_call | solution.py:496
  (171 shorter events, 77.9 us)
Async XLA Ops:
  2.5 29.4 %collective-permute-start.7 = (bf16[8,2,128,256]{3,2,1,0:T(8,128)(2,1)S(1)}, bf16[8,2,128,256]{3,2,1,0:T(8,128)(2,1)}, u32[]{:S(2)}, u32[]{:S(2)}) collective-permute-start(bf16[8,2,128,256]{3,2,1,0:T(8,128)(2,1)S(1)} %bitcast.21), channel_id=1, source_target_pairs={{0,8},{8,16},{16,24},{24,32},{32,40},{40,48},{48,56},{56,0},{64,72... | collective-permute-start | bytes 3145736 | tf_op jit(solution)/shard_map/ppermute | solution.py:302
  5.0 75.7 %collective-permute-start.8 = (bf16[8,2,128,256]{3,2,1,0:T(8,128)(2,1)S(1)}, bf16[8,2,128,256]{3,2,1,0:T(8,128)(2,1)}, u32[]{:S(2)}, u32[]{:S(2)}) collective-permute-start(bf16[8,2,128,256]{3,2,1,0:T(8,128)(2,1)S(1)} %bitcast.22), channel_id=1, source_target_pairs={{0,56},{8,0},{16,8},{24,16},{32,24},{40,32},{48,40},{56,48},{64,12... | collective-permute-start | bytes 3145736 | tf_op jit(solution)/shard_map/ppermute | solution.py:302
  9.1 72.4 %collective-permute-start = (bf16[8,2,128,256]{3,2,1,0:T(8,128)(2,1)S(1)}, bf16[8,2,128,256]{3,2,1,0:T(8,128)(2,1)}, u32[]{:S(2)}, u32[]{:S(2)}) collective-permute-start(bf16[8,2,128,256]{3,2,1,0:T(8,128)(2,1)S(1)} %bitcast.17), channel_id=1, source_target_pairs={{0,8},{8,16},{16,24},{24,32},{32,40},{40,48},{48,56},{56,0},{64,72... | collective-permute-start | bytes 3145736 | tf_op jit(solution)/shard_map/ppermute | solution.py:302
  9.2 73.0 %collective-permute-start.2 = (bf16[8,2,128,256]{3,2,1,0:T(8,128)(2,1)S(1)}, bf16[8,2,128,256]{3,2,1,0:T(8,128)(2,1)}, u32[]{:S(2)}, u32[]{:S(2)}) collective-permute-start(bf16[8,2,128,256]{3,2,1,0:T(8,128)(2,1)S(1)} %bitcast.18), channel_id=1, source_target_pairs={{0,56},{8,0},{16,8},{24,16},{32,24},{40,32},{48,40},{56,48},{64,12... | collective-permute-start | bytes 3145736 | tf_op jit(solution)/shard_map/ppermute | solution.py:302
  31.9 81.9 %collective-permute-start.16 = (bf16[8,2,128,256]{3,2,1,0:T(8,128)(2,1)}, bf16[8,2,128,256]{3,2,1,0:T(8,128)(2,1)S(1)}, u32[]{:S(2)}, u32[]{:S(2)}) collective-permute-start(bf16[8,2,128,256]{3,2,1,0:T(8,128)(2,1)} %collective-permute-done.7.l1_a.refs_1_), channel_id=1, source_target_pairs={{0,8},{8,16},{16,24},{24,32},{32,40},{40,48},{48,56},{56,0},{64,72... | collective-permute-start | bytes 3145736 | tf_op jit(solution)/shard_map/ppermute | solution.py:302
  53.8 25.7 %collective-permute-start.21 = (bf16[2,2,32,512]{3,2,1,0:T(8,128)(2,1)}, bf16[2,2,32,512]{3,2,1,0:T(8,128)(2,1)S(1)}, u32[]{:S(2)}, u32[]{:S(2)}) collective-permute-start(bf16[2,2,32,512]{3,2,1,0:T(8,128)(2,1)} %shard_map.81.refs_0_.refs_2_.refs_3_.refs_4_.refs_5_.refs_6_), channel_id=1, source_target_pairs={{0,8},{8,16},{16,24},{24,32},{32,40},{40,48},{48,56},{56,0},{64,72... | collective-permute-start | bytes 393224 | tf_op jit(solution)/shard_map/ppermute | solution.py:302
  80.7 33.5 %collective-permute-start.17 = (bf16[8,2,128,256]{3,2,1,0:T(8,128)(2,1)}, bf16[8,2,128,256]{3,2,1,0:T(8,128)(2,1)S(1)}, u32[]{:S(2)}, u32[]{:S(2)}) collective-permute-start(bf16[8,2,128,256]{3,2,1,0:T(8,128)(2,1)} %collective-permute-done.8.r1_a.refs_7_), channel_id=1, source_target_pairs={{0,56},{8,0},{16,8},{24,16},{32,24},{40,32},{48,40},{56,48},{64,12... | collective-permute-start | bytes 3145736 | tf_op jit(solution)/shard_map/ppermute | solution.py:302
  81.5 37.8 %collective-permute-start.1 = (bf16[8,2,128,256]{3,2,1,0:T(8,128)(2,1)}, bf16[8,2,128,256]{3,2,1,0:T(8,128)(2,1)}, u32[]{:S(2)}, u32[]{:S(2)}) collective-permute-start(bf16[8,2,128,256]{3,2,1,0:T(8,128)(2,1)} %collective-permute-done.l1_b.refs_1_), channel_id=1, source_target_pairs={{0,8},{8,16},{16,24},{24,32},{32,40},{40,48},{48,56},{56,0},{64,72... | collective-permute-start | bytes 3145736 | tf_op jit(solution)/shard_map/ppermute | solution.py:302
  82.2 49.5 %collective-permute-start.3 = (bf16[8,2,128,256]{3,2,1,0:T(8,128)(2,1)}, bf16[8,2,128,256]{3,2,1,0:T(8,128)(2,1)}, u32[]{:S(2)}, u32[]{:S(2)}) collective-permute-start(bf16[8,2,128,256]{3,2,1,0:T(8,128)(2,1)} %collective-permute-done.2.r1_b.refs_7_), channel_id=1, source_target_pairs={{0,56},{8,0},{16,8},{24,16},{32,24},{40,32},{48,40},{56,48},{64,12... | collective-permute-start | bytes 3145736 | tf_op jit(solution)/shard_map/ppermute | solution.py:302
  87.0 24.0 %collective-permute-start.23 = (bf16[2,2,32,512]{3,2,1,0:T(8,128)(2,1)}, bf16[2,2,32,512]{3,2,1,0:T(8,128)(2,1)S(1)}, u32[]{:S(2)}, u32[]{:S(2)}) collective-permute-start(bf16[2,2,32,512]{3,2,1,0:T(8,128)(2,1)} %shard_map.82.refs_0_.refs_1_.refs_7_), channel_id=1, source_target_pairs={{0,24},{8,32},{16,40},{24,48},{32,56},{40,0},{48,8},{56,16},{64,88... | collective-permute-start | bytes 393224 | tf_op jit(solution)/shard_map/ppermute | solution.py:302
  111.0 38.9 %collective-permute-start.10 = (bf16[8,2,128,256]{3,2,1,0:T(8,128)(2,1)}, bf16[8,2,128,256]{3,2,1,0:T(8,128)(2,1)}, u32[]{:S(2)}, u32[]{:S(2)}) collective-permute-start(bf16[8,2,128,256]{3,2,1,0:T(8,128)(2,1)} %get-tuple-element.29), channel_id=1, source_target_pairs={{0,192},{8,200},{16,208},{24,216},{32,224},{40,232},{48,240},{56,2... | collective-permute-start | bytes 3145736 | tf_op jit(solution)/shard_map/ppermute | solution.py:302
  119.3 36.3 %collective-permute-start.28 = (bf16[6,2,128,256]{3,2,1,0:T(8,128)(2,1)}, bf16[6,2,128,256]{3,2,1,0:T(8,128)(2,1)S(1)}, u32[]{:S(2)}, u32[]{:S(2)}) collective-permute-start(bf16[6,2,128,256]{3,2,1,0:T(8,128)(2,1)} %get-tuple-element.41), channel_id=1, source_target_pairs={{0,8},{8,16},{16,24},{24,32},{32,40},{40,48},{48,56},{56,0},{64,72... | collective-permute-start | bytes 2359304 | tf_op jit(solution)/shard_map/ppermute | solution.py:302
  131.7 24.0 %collective-permute-start.29 = (bf16[6,2,128,256]{3,2,1,0:T(8,128)(2,1)}, bf16[6,2,128,256]{3,2,1,0:T(8,128)(2,1)S(1)}, u32[]{:S(2)}, u32[]{:S(2)}) collective-permute-start(bf16[6,2,128,256]{3,2,1,0:T(8,128)(2,1)} %get-tuple-element.42), channel_id=1, source_target_pairs={{0,56},{8,0},{16,8},{24,16},{32,24},{40,32},{48,40},{56,48},{64,12... | collective-permute-start | bytes 2359304 | tf_op jit(solution)/shard_map/ppermute | solution.py:302
  135.1 34.8 %collective-permute-start.6 = (bf16[6,2,128,256]{3,2,1,0:T(8,128)(2,1)}, bf16[6,2,128,256]{3,2,1,0:T(8,128)(2,1)S(1)}, u32[]{:S(2)}, u32[]{:S(2)}) collective-permute-start(bf16[6,2,128,256]{3,2,1,0:T(8,128)(2,1)} %get-tuple-element.27), channel_id=1, source_target_pairs={{0,56},{8,0},{16,8},{24,16},{32,24},{40,32},{48,40},{56,48},{64,12... | collective-permute-start | bytes 2359304 | tf_op jit(solution)/shard_map/ppermute | solution.py:302
  135.2 56.7 %collective-permute-start.9 = (bf16[8,2,128,256]{3,2,1,0:T(8,128)(2,1)}, bf16[8,2,128,256]{3,2,1,0:T(8,128)(2,1)}, u32[]{:S(2)}, u32[]{:S(2)}) collective-permute-start(bf16[8,2,128,256]{3,2,1,0:T(8,128)(2,1)} %get-tuple-element.28), channel_id=1, source_target_pairs={{0,64},{8,72},{16,80},{24,88},{32,96},{40,104},{48,112},{56,120},{... | collective-permute-start | bytes 3145736 | tf_op jit(solution)/shard_map/ppermute | solution.py:302
  149.9 33.4 %collective-permute-start.4 = (bf16[6,2,128,256]{3,2,1,0:T(8,128)(2,1)}, bf16[6,2,128,256]{3,2,1,0:T(8,128)(2,1)S(1)}, u32[]{:S(2)}, u32[]{:S(2)}) collective-permute-start(bf16[6,2,128,256]{3,2,1,0:T(8,128)(2,1)} %get-tuple-element.26), channel_id=1, source_target_pairs={{0,8},{8,16},{16,24},{24,32},{32,40},{40,48},{48,56},{56,0},{64,72... | collective-permute-start | bytes 2359304 | tf_op jit(solution)/shard_map/ppermute | solution.py:302
  155.6 36.9 %collective-permute-start.25 = (bf16[3,2,128,256]{3,2,1,0:T(8,128)(2,1)}, bf16[3,2,128,256]{3,2,1,0:T(8,128)(2,1)S(1)}, u32[]{:S(2)}, u32[]{:S(2)}) collective-permute-start(bf16[3,2,128,256]{3,2,1,0:T(8,128)(2,1)} %get-tuple-element.38), channel_id=1, source_target_pairs={{0,64},{8,72},{16,80},{24,88},{32,96},{40,104},{48,112},{56,120},{... | collective-permute-start | bytes 1179656 | tf_op jit(solution)/shard_map/ppermute | solution.py:302
  155.7 36.8 %collective-permute-start.26 = (bf16[3,2,128,256]{3,2,1,0:T(8,128)(2,1)}, bf16[3,2,128,256]{3,2,1,0:T(8,128)(2,1)}, u32[]{:S(2)}, u32[]{:S(2)}) collective-permute-start(bf16[3,2,128,256]{3,2,1,0:T(8,128)(2,1)} %get-tuple-element.39), channel_id=1, source_target_pairs={{0,192},{8,200},{16,208},{24,216},{32,224},{40,232},{48,240},{56,2... | collective-permute-start | bytes 1179656 | tf_op jit(solution)/shard_map/ppermute | solution.py:302
  169.8 25.3 %collective-permute-start.35 = (bf16[2,2,128,256]{3,2,1,0:T(8,128)(2,1)}, bf16[2,2,128,256]{3,2,1,0:T(8,128)(2,1)}, u32[]{:S(2)}, u32[]{:S(2)}) collective-permute-start(bf16[2,2,128,256]{3,2,1,0:T(8,128)(2,1)} %slice.56), channel_id=1, source_target_pairs={{0,56},{8,0},{16,8},{24,16},{32,24},{40,32},{48,40},{56,48},{64,12... | collective-permute-start | bytes 786440 | tf_op jit(solution)/shard_map/ppermute | solution.py:302
  191.9 35.0 %collective-permute-start.30 = (bf16[4,2,128,256]{3,2,1,0:T(8,128)(2,1)}, bf16[4,2,128,256]{3,2,1,0:T(8,128)(2,1)S(1)}, u32[]{:S(2)}, u32[]{:S(2)}) collective-permute-start(bf16[4,2,128,256]{3,2,1,0:T(8,128)(2,1)} %get-tuple-element.43), channel_id=1, source_target_pairs={{0,64},{8,72},{16,80},{24,88},{32,96},{40,104},{48,112},{56,120},{... | collective-permute-start | bytes 1572872 | tf_op jit(solution)/shard_map/ppermute | solution.py:302
  199.2 30.5 %collective-permute-start.31 = (bf16[4,2,128,256]{3,2,1,0:T(8,128)(2,1)}, bf16[4,2,128,256]{3,2,1,0:T(8,128)(2,1)S(1)}, u32[]{:S(2)}, u32[]{:S(2)}) collective-permute-start(bf16[4,2,128,256]{3,2,1,0:T(8,128)(2,1)} %get-tuple-element.44), channel_id=1, source_target_pairs={{0,192},{8,200},{16,208},{24,216},{32,224},{40,232},{48,240},{56,2... | collective-permute-start | bytes 1572872 | tf_op jit(solution)/shard_map/ppermute | solution.py:302
  201.1 28.6 %collective-permute-start.32 = (bf16[4,2,128,256]{3,2,1,0:T(8,128)(2,1)}, bf16[4,2,128,256]{3,2,1,0:T(8,128)(2,1)S(1)}, u32[]{:S(2)}, u32[]{:S(2)}) collective-permute-start(bf16[4,2,128,256]{3,2,1,0:T(8,128)(2,1)} %get-tuple-element.45), channel_id=1, source_target_pairs={{0,128},{8,136},{16,144},{24,152},{32,160},{40,168},{48,176},{56,1... | collective-permute-start | bytes 1572872 | tf_op jit(solution)/shard_map/ppermute | solution.py:302
  218.6 28.9 %collective-permute-start.13 = (bf16[3,2,128,256]{3,2,1,0:T(8,128)(2,1)}, bf16[3,2,128,256]{3,2,1,0:T(8,128)(2,1)S(1)}, u32[]{:S(2)}, u32[]{:S(2)}) collective-permute-start(bf16[3,2,128,256]{3,2,1,0:T(8,128)(2,1)} %get-tuple-element.31), channel_id=1, source_target_pairs={{0,64},{8,72},{16,80},{24,88},{32,96},{40,104},{48,112},{56,120},{... | collective-permute-start | bytes 1179656 | tf_op jit(solution)/shard_map/ppermute | solution.py:302
  225.4 22.2 %collective-permute-start.14 = (bf16[3,2,128,256]{3,2,1,0:T(8,128)(2,1)}, bf16[3,2,128,256]{3,2,1,0:T(8,128)(2,1)S(1)}, u32[]{:S(2)}, u32[]{:S(2)}) collective-permute-start(bf16[3,2,128,256]{3,2,1,0:T(8,128)(2,1)} %get-tuple-element.32), channel_id=1, source_target_pairs={{0,192},{8,200},{16,208},{24,216},{32,224},{40,232},{48,240},{56,2... | collective-permute-start | bytes 1179656 | tf_op jit(solution)/shard_map/ppermute | solution.py:302
  (47 other events, 643.7 us)
